TPU v7x, 32 devices: a whole 2x2x4 slice. The times are simulated.
32 devices in a mesh: row: 4 (over z), col: 4 (over y, x), wave: 2 (over core).
Axes of the slice: x: 2, y: 2, z: 4, core: 2. Of those that a mesh axis runs over, the one named last changes fastest.
Arguments:
- transmission: float32 [4096, 4096], P('row', 'col'), may hold values from 0 to 1
- dual_focal: float32 [512, 8, 512], P(('row', 'col'), 'wave'), may hold values from -12 to 12
- dual_curvature: float32 [4096, 4096], P('row', 'col'), may hold values from -6 to 6
- pupil_mask: int32 [4096, 4096], P('row', 'col'), may hold values 0 or 1
- lyot_mask: int32 [4096, 4096], P('row', 'col'), may hold values 0 or 1
- dark_mask: int32 [512, 8, 512], P(('row', 'col'), 'wave'), may hold values 0 or 1
- focal_rows: float32 [8, 512, 4096], P('wave', None, 'row'), may hold values from -0.09375 to 0.09375
- focal_cols: float32 [8, 512, 4096], P('wave', None, 'col'), may hold values from -0.09375 to 0.09375
Outputs:
- transmission_out: float32 [4096, 4096], P('row', 'col')
- dual_focal_out: float32 [512, 8, 512], P(('row', 'col'), 'wave')
- dual_curvature_out: float32 [4096, 4096], P('row', 'col')
All inputs are finite; a program needn't handle non-finite values. No bound on the sum of `pupil_mask` or of `lyot_mask` or of `dark_mask` on one device may be relied on, other than what follows from the above.
Results may differ from a plain program's by a relative error of at most 0.0001.
Values sent between devices are 32-bit elements; how exact they have to be, the bound alone decides.
A program may use at most 128 MiB of HBM per device.

v0:
```python
import jax
import jax.numpy as jnp
from jax import lax
from jax.sharding import PartitionSpec as P

ITERS = 2


step_primal = 0.12
step_dual = 0.2
contrast = 0.5
curvature_limit = 0.1
highest = lax.Precision.HIGHEST


def padded_2(cells, sides, width):
    for axis, dim in sides:
        count = lax.axis_size(axis)
        ends = count - 1
        head = lax.slice_in_dim(cells, 0, width, axis=dim)
        tail = lax.slice_in_dim(cells, cells.shape[dim] - width, cells.shape[dim], axis=dim)
        cells = jnp.concatenate(
            [
                lax.ppermute(tail, axis, [(i, (i + 1) % count) for i in range(ends)]),
                cells,
                lax.ppermute(head, axis, [((i + 1) % count, i) for i in range(ends)]),
            ],
            axis=dim,
        )
    return cells


def around_sum(padded, field):
    beside_all = padded[2:, 1:-1] + padded[:-2, 1:-1] + padded[1:-1, 2:] + padded[1:-1, :-2]
    return 0.25 * beside_all - field


def fold_rows(focal_rows, carried):
    return jnp.einsum("wkr,kwc->rc", focal_rows, carried, precision=highest)


def per_device(
    transmission,
    dual_focal,
    dual_curvature,
    pupil_mask,
    lyot_mask,
    dark_mask,
    focal_rows,
    focal_cols,
):
    pupil = pupil_mask.astype(jnp.float32)
    stop = pupil * lyot_mask.astype(jnp.float32)
    dark = dark_mask.astype(jnp.float32)
    primal = transmission
    dual_f = dual_focal * dark
    dual_c = dual_curvature
    for iteration in range(ITERS):
        carried = jnp.einsum(
            "kwz,wzc->kwc",
            lax.all_gather(dual_f, ("row", "col"), axis=0, tiled=True),
            focal_cols,
            precision=highest,
        )
        backward = fold_rows(focal_rows, carried)
        total_back = lax.psum(backward, "wave")
        dual_padded = padded_2(dual_c, (("row", 0), ("col", 1)), 1)
        gradient = -pupil + stop * total_back + around_sum(dual_padded, dual_c)
        primal_new = jnp.clip(primal - step_primal * gradient, 0.0, 1.0)
        extended = 2.0 * primal_new - primal
        masked = stop * extended
        left_part = jnp.einsum("wkr,rc->kwc", focal_rows, masked, precision=highest)
        fields = lax.psum_scatter(
            jnp.einsum("kwc,wzc->kwz", left_part, focal_cols, precision=highest),
            ("row", "col"),
            scatter_dimension=0,
            tiled=True,
        )
        shifted = dual_f + step_dual * fields
        dual_f = dark * (shifted - step_dual * jnp.clip(shifted / step_dual, -contrast, contrast))
        primal_padded = padded_2(extended, (("row", 0), ("col", 1)), 1)
        moved = dual_c + step_dual * around_sum(primal_padded, extended)
        dual_c = moved - step_dual * jnp.clip(moved / step_dual, -curvature_limit, curvature_limit)
        primal = primal_new
    return (primal, dual_f, dual_c)


def solution(mesh):
    return jax.shard_map(
        per_device,
        mesh=mesh,
        in_specs=(
            P("row", "col"),
            P(("row", "col"), "wave", None),
            P("row", "col"),
            P("row", "col"),
            P("row", "col"),
            P(("row", "col"), "wave", None),
            P("wave", None, "row"),
            P("wave", None, "col"),
        ),
        out_specs=(P("row", "col"), P(("row", "col"), "wave", None), P("row", "col")),
        check_vma=False,
    )
```

profile of v0, /device:TPU:0, one launch (start us, length us, event | category | flops | bytes accessed | tf_op | source)
XLA Modules:
  0.0 738.3 jit_solution(1173187141930892320)
XLA Ops:
  9.2 80.4 %all-gather.3.cloned.1.call-done = f32[512,4,512]{2,0,1:T(8,128)} async-done(((f32[32,4,512]{2,0,1:T(8,128)}), f32[512,4,512]{2,0,1:T(8,128)}) %all-gather.3.cloned.1.call-update) | async-done | bytes 4194320 | tf_op jit(solution)/shard_map/all_gather | solution.py:61
  89.6 17.2 %fusion.58 = f32[4,512,1024]{1,2,0:T(8,128)S(1)} fusion(f32[512,4,512]{2,0,1:T(8,128)} %all-gather.3.cloned.1.call-done, f32[4,512,1024]{2,1,0:T(8,128)} %param.15), kind=kOutput, calls=%fused_computation.80 | convolution fusion | flops 12884901888 | bytes 20971520 | tf_op jit(solution)/shard_map/kwz,wzc->kwc/dot_general | solution.py:59
  106.8 34.9 %fusion.42 = f32[1024,1024]{0,1:T(8,128)} fusion(f32[4,512,1024]{2,1,0:T(8,128)} %param.14, f32[4,512,1024]{1,2,0:T(8,128)S(1)} %fusion.58), kind=kOutput, calls=%fused_computation.64 | convolution fusion | flops 25769803776 | bytes 20971520 | tf_op jit(solution)/shard_map/wkr,kwc->rc/dot_general | solution.py:39
  147.7 5.6 copy.16
  160.5 6.9 concatenate.66
  190.5 20.2 %multiply_subtract_fusion.3 = (f32[1024,1024]{0,1:T(8,128)}, f32[1024,1024]{0,1:T(8,128)}, f32[1024,1024]{0,1:T(8,128)}) fusion(f32[1024,1024]{0,1:T(8,128)} %copy.21, f32[1024,1024]{0,1:T(8,128)} %copy.16, f32[1026,1024]{0,1:T(8,128)} %concatenate.66, f32[1026,1]{0,1:T(1,128)S(1)} %collective-permute-done.3, f32[1026,1]{0,1:T(1,128)S(1)} %collective-permute-done.2, ...), kind=kLoop, calls=%fused_computation.61 | loop fusion | flops 22020096 | bytes 37773328 | tf_op jit(solution)/shard_map/sub | solution.py:70
  210.6 30.5 %fusion.38 = f32[1024,4,512]{0,2,1:T(8,128)S(1)} fusion(f32[4,512,1024]{2,1,0:T(8,128)} %param.14, f32[1024,1024]{0,1:T(8,128)} %get-tuple-element.10, f32[1024,1024]{0,1:T(8,128)} %get-tuple-element.8), kind=kOutput, calls=%fused_computation.54 | convolution fusion | flops 25770852352 | bytes 25165824 | tf_op jit(solution)/shard_map/wkr,rc->kwc/dot_general | solution.py:72
  241.2 17.8 %convolution_bitcast_fusion.1 = f32[512,4,512]{2,0,1:T(8,128)} fusion(f32[1024,4,512]{0,2,1:T(8,128)S(1)} %fusion.38, f32[4,512,1024]{2,1,0:T(8,128)} %param.15), kind=kOutput, calls=%fused_computation.67 | convolution fusion | flops 12884901888 | bytes 20971520 | tf_op jit(solution)/shard_map/kwc,wzc->kwz/dot_general | solution.py:74
  259.0 94.2 %reduce-scatter.3.cloned.1.call-done = f32[32,4,512]{2,0,1:T(8,128)} async-done(((f32[512,4,512]{2,0,1:T(8,128)}), f32[32,4,512]{2,0,1:T(8,128)}) %reduce-scatter.3.cloned.1.call-update) | async-done | bytes 262160 | tf_op jit(solution)/shard_map/reduce_scatter | solution.py:73
  355.2 76.4 %all-gather.5.cloned.1.call-done = f32[512,4,512]{2,0,1:T(8,128)} async-done(((f32[32,4,512]{2,0,1:T(8,128)}), f32[512,4,512]{2,0,1:T(8,128)}) %all-gather.5.cloned.1.call-update) | async-done | bytes 4194320 | tf_op jit(solution)/shard_map/all_gather | solution.py:61
  431.5 17.3 %fusion.59 = f32[4,512,1024]{1,2,0:T(8,128)S(1)} fusion(f32[512,4,512]{2,0,1:T(8,128)} %all-gather.5.cloned.1.call-done, f32[4,512,1024]{2,1,0:T(8,128)} %param.15), kind=kOutput, calls=%fused_computation.81 | convolution fusion | flops 12884901888 | bytes 20971520 | tf_op jit(solution)/shard_map/kwz,wzc->kwc/dot_general | solution.py:59
  448.9 34.9 %fusion.45 = f32[1024,1024]{0,1:T(8,128)} fusion(f32[4,512,1024]{2,1,0:T(8,128)} %param.14, f32[4,512,1024]{1,2,0:T(8,128)S(1)} %fusion.59), kind=kOutput, calls=%fused_computation.65 | convolution fusion | flops 25769803776 | bytes 20971520 | tf_op jit(solution)/shard_map/wkr,kwc->rc/dot_general | solution.py:39
  491.1 8.2 %collective-permute-done.4 = f32[1,1024]{0,1:T(8,128)S(1)} collective-permute-done((f32[1,1024]{0,1:T(8,128)S(1)}, f32[1,1024]{0,1:T(8,128)S(1)}, u32[]{:S(2)}, u32[]{:S(2)}) %collective-permute-start.4) | collective-permute-done | bytes 4128 | tf_op jit(solution)/shard_map/ppermute | solution.py:26
  500.6 6.7 concatenate.71
  515.2 15.7 %multiply_subtract_fusion.2 = f32[1024,1024]{0,1:T(8,128)S(1)} fusion(f32[1024,1024]{0,1:T(8,128)} %copy.16, f32[1024,1024]{0,1:T(8,128)} %get-tuple-element.8, f32[1026,1024]{0,1:T(8,128)} %concatenate.71, f32[1026,1]{0,1:T(1,128)S(1)} %collective-permute-done.7, f32[1026,1]{0,1:T(1,128)S(1)} %collective-permute-done.6, ...), kind=kLoop, calls=%fused_computation.59 | loop fusion | flops 15728640 | bytes 16801808 | tf_op jit(solution)/shard_map/sub | solution.py:83
  539.5 6.1 collective-permute-done.8
  546.8 6.4 concatenate.76
  561.5 17.9 %multiply_subtract_fusion.1 = (f32[1024,1024]{0,1:T(8,128)S(1)}, f32[1024,1024]{0,1:T(8,128)}) fusion(f32[1024,1024]{0,1:T(8,128)} %get-tuple-element.9, f32[1024,1024]{0,1:T(8,128)} %copy-done, f32[1026,1024]{0,1:T(8,128)} %concatenate.76, f32[1026,1]{0,1:T(1,128)S(1)} %collective-permute-done.11, f32[1026,1]{0,1:T(1,128)S(1)} %collective-permute-done.10, ...), kind=kLoop, calls=%fused_computation.58 | loop fusion | flops 19922944 | bytes 33579024 | tf_op jit(solution)/shard_map/sub | solution.py:70
  579.4 31.8 %fusion.36 = f32[1024,4,512]{0,2,1:T(8,128)S(1)} fusion(f32[4,512,1024]{2,1,0:T(8,128)} %param.14, f32[1024,1024]{0,1:T(8,128)} %get-tuple-element.10, f32[1024,1024]{0,1:T(8,128)S(1)} %get-tuple-element.6), kind=kOutput, calls=%fused_computation.52 | convolution fusion | flops 25770852352 | bytes 25165824 | tf_op jit(solution)/shard_map/wkr,rc->kwc/dot_general | solution.py:72
  611.3 17.4 %convolution_bitcast_fusion = f32[512,4,512]{2,0,1:T(8,128)} fusion(f32[1024,4,512]{0,2,1:T(8,128)S(1)} %fusion.36, f32[4,512,1024]{2,1,0:T(8,128)} %param.15), kind=kOutput, calls=%fused_computation.66 | convolution fusion | flops 12884901888 | bytes 20971520 | tf_op jit(solution)/shard_map/kwc,wzc->kwz/dot_general | solution.py:74
  645.9 6.4 concatenate.81
  659.0 5.6 copy.24
  664.6 17.0 %multiply_subtract_fusion = f32[1024,1024]{0,1:T(8,128)} fusion(f32[1024,1024]{0,1:T(8,128)} %copy-done, f32[1024,1024]{0,1:T(8,128)} %copy-done.1, f32[1026,1024]{0,1:T(8,128)} %concatenate.81, f32[1026,1]{0,1:T(1,128)S(1)} %collective-permute-done.15, f32[1026,1]{0,1:T(1,128)S(1)} %collective-permute-done.14, f32[1,1024]{0,1:T(8,128)S(1)} %collective-permute-done.13, ...), kind=kLoop, calls=%fused_computation.56 | loop fusion | flops 15728640 | bytes 16801808 | tf_op jit(solution)/shard_map/sub | solution.py:83
  687.0 42.3 %reduce-scatter.5.cloned.1.call-done = f32[32,4,512]{2,0,1:T(8,128)} async-done(((f32[512,4,512]{2,0,1:T(8,128)}), f32[32,4,512]{2,0,1:T(8,128)}) %reduce-scatter.5.cloned.1.call-update) | async-done | bytes 262160 | tf_op jit(solution)/shard_map/reduce_scatter | solution.py:73
  (72 shorter events, 106.0 us)
Async XLA Ops:
  7.2 82.4 %all-gather.3.cloned.1.call-start = ((), (), s32[]{:S(2)}) async-start(), calls=%async_computation.2 | async-start | bytes 4456448 | tf_op jit(solution)/shard_map/all_gather | solution.py:61
  9.1 181.3 %all-reduce.3.cloned.1.call-start = ((), (), s32[]{:S(2)}) async-start(), calls=%async_computation.3 | async-start | bytes 8388608 | tf_op jit(solution)/shard_map/psum | solution.py:66
  141.7 211.5 %reduce-scatter.3.cloned.1.call-start = ((), (), s32[]{:S(2)}) async-start(), calls=%async_computation.4 | async-start | bytes 4456448 | tf_op jit(solution)/shard_map/reduce_scatter | solution.py:73
  142.8 13.4 %collective-permute-start.1 = (f32[1,1024]{0,1:T(8,128)S(1)}, f32[1,1024]{0,1:T(8,128)S(1)}, u32[]{:S(2)}, u32[]{:S(2)}) collective-permute-start(f32[1,1024]{0,1:T(8,128)S(1)} %copy.17), channel_id=1, source_target_pairs={{0,8},{8,16},{16,24},{1,9},{9,17},{17,25},{2,10},{10,18},{18,26},{... | collective-permute-start | bytes 12296 | tf_op jit(solution)/shard_map/ppermute | solution.py:24
  146.4 14.1 %collective-permute-start = (f32[1,1024]{0,1:T(8,128)S(1)}, f32[1,1024]{0,1:T(8,128)S(1)}, u32[]{:S(2)}, u32[]{:S(2)}) collective-permute-start(f32[1,1024]{0,1:T(8,128)S(1)} %copy.15), channel_id=1, source_target_pairs={{8,0},{16,8},{24,16},{9,1},{17,9},{25,17},{10,2},{18,10},{26,18},{... | collective-permute-start | bytes 12296 | tf_op jit(solution)/shard_map/ppermute | solution.py:26
  168.2 22.2 %collective-permute-start.2 = (f32[1026,1]{0,1:T(1,128)S(1)}, f32[1026,1]{0,1:T(1,128)S(1)}, u32[]{:S(2)}, u32[]{:S(2)}) collective-permute-start(f32[1026,1]{0,1:T(1,128)S(1)} %get-tuple-element.17), channel_id=1, source_target_pairs={{2,0},{4,2},{6,4},{3,1},{5,3},{7,5},{10,8},{12,10},{14,12},{11,9},... | collective-permute-start | bytes 12320 | tf_op jit(solution)/shard_map/ppermute | solution.py:26
  169.5 20.9 %collective-permute-start.3 = (f32[1026,1]{0,1:T(1,128)S(1)}, f32[1026,1]{0,1:T(1,128)S(1)}, u32[]{:S(2)}, u32[]{:S(2)}) collective-permute-start(f32[1026,1]{0,1:T(1,128)S(1)} %get-tuple-element.18), channel_id=1, source_target_pairs={{0,2},{2,4},{4,6},{1,3},{3,5},{5,7},{8,10},{10,12},{12,14},{9,11},... | collective-permute-start | bytes 12320 | tf_op jit(solution)/shard_map/ppermute | solution.py:24
  258.9 94.3 %copy-start.2 = (s32[32,4,512]{2,1,0:T(4,128)S(1)}, s32[32,4,512]{2,1,0:T(4,128)}, u32[]{:S(2)}) copy-start(s32[32,4,512]{2,1,0:T(4,128)} %param.13) | copy-start | bytes 786436
  258.9 94.3 %copy-start.4 = (f32[32,4,512]{2,1,0:T(4,128)S(1)}, f32[32,4,512]{2,1,0:T(4,128)}, u32[]{:S(2)}) copy-start(f32[32,4,512]{2,1,0:T(4,128)} %param.9) | copy-start | bytes 786436
  258.9 172.6 %all-gather.5.cloned.1.call-start = ((), (), s32[]{:S(2)}) async-start(), calls=%async_computation.5 | async-start | bytes 4456448 | tf_op jit(solution)/shard_map/all_gather | solution.py:61
  355.1 206.4 %all-reduce.5.cloned.1.call-start = ((), (), s32[]{:S(2)}) async-start(), calls=%async_computation.6 | async-start | bytes 8388608 | tf_op jit(solution)/shard_map/psum | solution.py:66
  483.8 245.5 %reduce-scatter.5.cloned.1.call-start = ((), (), s32[]{:S(2)}) async-start(), calls=%async_computation.7 | async-start | bytes 4456448 | tf_op jit(solution)/shard_map/reduce_scatter | solution.py:73
  485.3 14.1 %collective-permute-start.4 = (f32[1,1024]{0,1:T(8,128)S(1)}, f32[1,1024]{0,1:T(8,128)S(1)}, u32[]{:S(2)}, u32[]{:S(2)}) collective-permute-start(f32[1,1024]{0,1:T(8,128)S(1)} %get-tuple-element.23), channel_id=1, source_target_pairs={{8,0},{16,8},{24,16},{9,1},{17,9},{25,17},{10,2},{18,10},{26,18},{... | collective-permute-start | bytes 12296 | tf_op jit(solution)/shard_map/ppermute | solution.py:26
  486.6 14.0 %collective-permute-start.5 = (f32[1,1024]{0,1:T(8,128)S(1)}, f32[1,1024]{0,1:T(8,128)S(1)}, u32[]{:S(2)}, u32[]{:S(2)}) collective-permute-start(f32[1,1024]{0,1:T(8,128)S(1)} %get-tuple-element.24), channel_id=1, source_target_pairs={{0,8},{8,16},{16,24},{1,9},{9,17},{17,25},{2,10},{10,18},{18,26},{... | collective-permute-start | bytes 12296 | tf_op jit(solution)/shard_map/ppermute | solution.py:24
  508.0 5.8 collective-permute-start.6
  509.3 5.9 collective-permute-start.7
  533.1 12.5 %collective-permute-start.8 = (f32[1,1024]{0,1:T(8,128)S(1)}, f32[1,1024]{0,1:T(8,128)S(1)}, u32[]{:S(2)}, u32[]{:S(2)}) collective-permute-start(f32[1,1024]{0,1:T(8,128)S(1)} %get-tuple-element.21), channel_id=1, source_target_pairs={{8,0},{16,8},{24,16},{9,1},{17,9},{25,17},{10,2},{18,10},{26,18},{... | collective-permute-start | bytes 12296 | tf_op jit(solution)/shard_map/ppermute | solution.py:26
  534.4 12.4 %collective-permute-start.9 = (f32[1,1024]{0,1:T(8,128)S(1)}, f32[1,1024]{0,1:T(8,128)S(1)}, u32[]{:S(2)}, u32[]{:S(2)}) collective-permute-start(f32[1,1024]{0,1:T(8,128)S(1)} %get-tuple-element.22), channel_id=1, source_target_pairs={{0,8},{8,16},{16,24},{1,9},{9,17},{17,25},{2,10},{10,18},{18,26},{... | collective-permute-start | bytes 12296 | tf_op jit(solution)/shard_map/ppermute | solution.py:24
  554.0 6.2 collective-permute-start.10
  555.3 6.2 collective-permute-start.11
  630.1 11.5 %collective-permute-start.12 = (f32[1,1024]{0,1:T(8,128)S(1)}, f32[1,1024]{0,1:T(8,128)S(1)}, u32[]{:S(2)}, u32[]{:S(2)}) collective-permute-start(f32[1,1024]{0,1:T(8,128)S(1)} %get-tuple-element.19), channel_id=1, source_target_pairs={{8,0},{16,8},{24,16},{9,1},{17,9},{25,17},{10,2},{18,10},{26,18},{... | collective-permute-start | bytes 12296 | tf_op jit(solution)/shard_map/ppermute | solution.py:26
  631.4 14.5 %collective-permute-start.13 = (f32[1,1024]{0,1:T(8,128)S(1)}, f32[1,1024]{0,1:T(8,128)S(1)}, u32[]{:S(2)}, u32[]{:S(2)}) collective-permute-start(f32[1,1024]{0,1:T(8,128)S(1)} %get-tuple-element.20), channel_id=1, source_target_pairs={{0,8},{8,16},{16,24},{1,9},{9,17},{17,25},{2,10},{10,18},{18,26},{... | collective-permute-start | bytes 12296 | tf_op jit(solution)/shard_map/ppermute | solution.py:24
  653.1 11.5 %collective-permute-start.14 = (f32[1026,1]{0,1:T(1,128)S(1)}, f32[1026,1]{0,1:T(1,128)S(1)}, u32[]{:S(2)}, u32[]{:S(2)}) collective-permute-start(f32[1026,1]{0,1:T(1,128)S(1)} %get-tuple-element.11), channel_id=1, source_target_pairs={{2,0},{4,2},{6,4},{3,1},{5,3},{7,5},{10,8},{12,10},{14,12},{11,9},... | collective-permute-start | bytes 12320 | tf_op jit(solution)/shard_map/ppermute | solution.py:26
  654.4 10.2 %collective-permute-start.15 = (f32[1026,1]{0,1:T(1,128)S(1)}, f32[1026,1]{0,1:T(1,128)S(1)}, u32[]{:S(2)}, u32[]{:S(2)}) collective-permute-start(f32[1026,1]{0,1:T(1,128)S(1)} %get-tuple-element.12), channel_id=1, source_target_pairs={{0,2},{2,4},{4,6},{1,3},{3,5},{5,7},{8,10},{10,12},{12,14},{9,11},... | collective-permute-start | bytes 12320 | tf_op jit(solution)/shard_map/ppermute | solution.py:24
  (3 other events, 81.6 us)
Sparse Core Ops, SparseCore 0:
  11.3 78.2 all-gather.2
  141.8 26.6 all-reduce.2
  259.1 94.1 reduce-scatter.2
  356.4 75.0 all-gather.4
  483.9 26.6 all-reduce.4
  628.8 100.4 reduce-scatter.4
where the time goes:
time: 748 us; the launch traced here: 738 us
  waiting for transfers between devices  329 us (44%)
  matrix products  202 us (27%)
  other arithmetic  75.6 us (10%)
  local copies, waits for them, and re-layouts  69.5 us (9%)
  starting transfers between devices  47.4 us (6%)
  between operations  14.6 us (2%)
    all_gather x2, waiting for transfers between devices, per_device(): lax.all_gather(dual_f, ('row', 'col'), axis=0, tiled=True)  157 us
    reduce_scatter x2, waiting for transfers between devices, per_device(): lax.psum_scatter(jnp.einsum('kwc,wzc->kwz', left_part, focal_cols, precis...  137 us
    dot_general x2, matrix products, fold_rows(): return jnp.einsum('wkr,kwc->rc', focal_rows, carried, precision=highest)  69.8 us
    dot_general x2, matrix products, per_device(): left_part = jnp.einsum('wkr,rc->kwc', focal_rows, masked, precision=highest)  62.3 us
    sub x2, other arithmetic, per_device(): extended = 2.0 * primal_new - primal  38.1 us
    ppermute x8, starting transfers between devices, padded_2(): lax.ppermute(tail, axis, [(i, (i + 1) % count) for i in range(ends)])  36.9 us
    unnamed x17, local copies, waits for them, and re-layouts  35.7 us
    dot_general x2, matrix products, per_device(): jnp.einsum('kwc,wzc->kwz', left_part, focal_cols, precision=highest)  35.1 us
  transfers between devices with their start and end apart: 22, of which 14 were waited for; matrix products, arithmetic and copies ran while one was open for 13% of the time, Pallas kernels for 0%

commit v1 on v0

v1 whole, which is shorter than its diff:
```python
import functools

import jax
import jax.numpy as jnp
from jax import lax
from jax.experimental import pallas as pl
from jax.experimental.pallas import tpu as pltpu
from jax.sharding import PartitionSpec as P

ITERS = 2
step_primal = 0.12
step_dual = 0.2
contrast = 0.5
curvature_limit = 0.1
high = lax.Precision.HIGH
CHUNKS = 2


def around(v, above8, below8, top, bottom, left, right):
    i, last = pl.program_id(0), pl.num_programs(0) - 1
    up = jnp.where(i == 0, top[...], above8[7:8, :])
    down = jnp.where(i == last, bottom[...], below8[0:1, :])
    rows, cols = v.shape
    r = lax.broadcasted_iota(jnp.int32, v.shape, 0)
    c = lax.broadcasted_iota(jnp.int32, v.shape, 1)
    from_up = jnp.where(r == 0, up, pltpu.roll(v, 1, 0))
    from_down = jnp.where(r == rows - 1, down, pltpu.roll(v, rows - 1, 0))
    from_left = jnp.where(c == 0, left[...], pltpu.roll(v, 1, 1))
    from_right = jnp.where(c == cols - 1, right[...], pltpu.roll(v, cols - 1, 1))
    return 0.25 * (from_down + from_up + from_right + from_left) - v


def primal_kernel(mine, other, primal, pupil_m, lyot_m, dual, above, below, top, bottom, left, right, new_ref, ext_ref, mask_ref):
    pupil = pupil_m[...].astype(jnp.float32)
    stop = pupil * lyot_m[...].astype(jnp.float32)
    x = primal[...]
    curv = around(dual[...], above, below, top, bottom, left, right)
    gradient = stop * (mine[...] + other[...]) - pupil + curv
    new = jnp.clip(x - step_primal * gradient, 0.0, 1.0)
    ext = 2.0 * new - x
    new_ref[...] = new
    ext_ref[...] = ext
    mask_ref[...] = stop * ext


def dual_kernel(dual, ext, above, below, top, bottom, left, right, out_ref):
    moved = dual[...] + step_dual * around(ext[...], above, below, top, bottom, left, right)
    out_ref[...] = moved - step_dual * jnp.clip(moved / step_dual, -curvature_limit, curvature_limit)


def specs(rows, cols, block):
    steps, eights = rows // block, block // 8
    whole = pl.BlockSpec((block, cols), lambda i: (i, 0))
    halo = [
        pl.BlockSpec((8, cols), lambda i: (jnp.maximum(i * eights - 1, 0), 0)),
        pl.BlockSpec((8, cols), lambda i: (jnp.minimum((i + 1) * eights, steps * eights - 1), 0)),
        pl.BlockSpec((1, cols), lambda i: (0, 0)),
        pl.BlockSpec((1, cols), lambda i: (0, 0)),
        pl.BlockSpec((block, 1), lambda i: (i, 0)),
        pl.BlockSpec((block, 1), lambda i: (i, 0)),
    ]
    return steps, whole, halo


def primal_step(mine, other, primal, pupil, lyot, dual, edges):
    rows, cols = primal.shape
    steps, whole, halo = specs(rows, cols, 128)
    out = jax.ShapeDtypeStruct((rows, cols), jnp.float32)
    return pl.pallas_call(
        primal_kernel,
        grid=(steps,),
        in_specs=[whole] * 6 + halo,
        out_specs=[whole] * 3,
        out_shape=[out] * 3,
        cost_estimate=pl.CostEstimate(flops=30 * rows * cols, bytes_accessed=36 * rows * cols, transcendentals=0),
    )(mine, other, primal, pupil, lyot, dual, dual, dual, *edges)


def dual_step(dual, ext, edges):
    rows, cols = dual.shape
    steps, whole, halo = specs(rows, cols, 128)
    return pl.pallas_call(
        dual_kernel,
        grid=(steps,),
        in_specs=[whole] * 2 + halo,
        out_specs=whole,
        out_shape=jax.ShapeDtypeStruct((rows, cols), jnp.float32),
        cost_estimate=pl.CostEstimate(flops=20 * rows * cols, bytes_accessed=12 * rows * cols, transcendentals=0),
    )(dual, ext, ext, ext, *edges)


def edges_of(v):
    out = []
    for axis, dim in (("row", 0), ("col", 1)):
        count = lax.axis_size(axis)
        head = lax.slice_in_dim(v, 0, 1, axis=dim)
        tail = lax.slice_in_dim(v, v.shape[dim] - 1, v.shape[dim], axis=dim)
        out.append(lax.ppermute(tail, axis, [(i, i + 1) for i in range(count - 1)]))
        out.append(lax.ppermute(head, axis, [(i + 1, i) for i in range(count - 1)]))
    return out


def gather(part):
    return lax.all_gather(part, ("row", "col"), axis=0, tiled=True)


def scatter(part):
    return lax.psum_scatter(part, ("row", "col"), scatter_dimension=0, tiled=True)


def other_waves(part):
    n = lax.axis_size("wave")
    if n == 1:
        return jnp.zeros_like(part)
    if n == 2:
        return lax.ppermute(part, "wave", [(0, 1), (1, 0)])
    return lax.psum(part, "wave") - part


def per_device(transmission, dual_focal, dual_curvature, pupil_mask, lyot_mask, dark_mask, focal_rows, focal_cols):
    dark = dark_mask.astype(jnp.float32)
    waves = dark.shape[1]
    chunks = CHUNKS if waves % CHUNKS == 0 else 1
    size = waves // chunks
    pieces = [slice(n * size, (n + 1) * size) for n in range(chunks)]
    darks = [dark[:, p] for p in pieces]
    duals = [dual_focal[:, p] * d for p, d in zip(pieces, darks)]
    rows_of = [focal_rows[p] for p in pieces]
    cols_of = [focal_cols[p] for p in pieces]
    primal, dual_c = transmission, dual_curvature
    fulls = [gather(d) for d in duals]
    for iteration in range(ITERS):
        dual_edges = edges_of(dual_c)
        carried = [jnp.einsum("kwz,wzc->kwc", f, c, precision=high) for f, c in zip(fulls, cols_of)]
        backward = functools.reduce(
            jnp.add, [jnp.einsum("wkr,kwc->rc", r, c, precision=high) for r, c in zip(rows_of, carried)]
        )
        other = other_waves(backward)
        primal, extended, masked = primal_step(backward, other, primal, pupil_mask, lyot_mask, dual_c, dual_edges)
        new_duals = []
        fulls = []
        for r, c, d, k in zip(rows_of, cols_of, duals, darks):
            left = jnp.einsum("wkr,rc->kwc", r, masked, precision=high)
            fields = scatter(jnp.einsum("kwc,wzc->kwz", left, c, precision=high))
            shifted = d + step_dual * fields
            new = k * (shifted - step_dual * jnp.clip(shifted / step_dual, -contrast, contrast))
            new_duals.append(new)
            if iteration < ITERS - 1:
                fulls.append(gather(new))
        duals = new_duals
        dual_c = dual_step(dual_c, extended, edges_of(extended))
    return (primal, jnp.concatenate(duals, axis=1), dual_c)


def solution(mesh):
    return jax.shard_map(
        per_device,
        mesh=mesh,
        in_specs=(
            P("row", "col"),
            P(("row", "col"), "wave", None),
            P("row", "col"),
            P("row", "col"),
            P("row", "col"),
            P(("row", "col"), "wave", None),
            P("wave", None, "row"),
            P("wave", None, "col"),
        ),
        out_specs=(P("row", "col"), P(("row", "col"), "wave", None), P("row", "col")),
        check_vma=False,
    )
```

time: 748 us -> 822 us (1.099)
  waiting for transfers between devices: 329 us -> 532 us
  matrix products: 202 us -> 129 us
  other arithmetic: 75.6 us -> 4.62 us
  Pallas kernels: 0 us -> 52.1 us
  local copies, waits for them, and re-layouts: 69.5 us -> 17.6 us
  starting transfers between devices: 47.4 us -> 61.6 us
    reduce_scatter x2 -> x4, waiting for transfers between devices: 137 us -> 263 us  [scatter(): lax.psum_scatter(part, ('row', 'col'), scatter_dimension=0, tiled=True)]
    dot_general x8 -> x16, matrix products: 202 us -> 129 us  [the longest x4 39.3 us: per_device(): left = jnp.einsum('wkr,rc->kwc', r, masked, precision=high)]
    sub x4 -> x0, other arithmetic: 70.7 us -> none  [the longest x2 38.1 us: per_device(): extended = 2.0 * primal_new - primal]
    all_gather x2 -> x4, waiting for transfers between devices: 157 us -> 214 us  [gather(): return lax.all_gather(part, ('row', 'col'), axis=0, tiled=True)]
    pallas_call x0 -> x4, Pallas kernels: none -> 52.1 us  [the longest x2 33.3 us: primal_step(): pl.pallas_call(primal_kernel, grid=(steps,), in_specs=[whole] * 6 + halo,...]
    unnamed x17 -> x49, local copies, waits for them, and re-layouts: 35.7 us -> 7.65 us
    concatenate x4 -> x0, local copies, waits for them, and re-layouts: 26.4 us -> none  [padded_2(): jnp.concatenate([lax.ppermute(tail, axis, [(i, (i + 1) % count) for i in...]
    ppermute x16 -> x18, waiting for transfers between devices: 36 us -> 53.8 us  [the longest x8 53.4 us: edges_of(): out.append(lax.ppermute(head, axis, [(i + 1, i) for i in range(count - 1)]))]
  transfers between devices with their start and end apart: 22 -> 26, of which waited for: 14 -> 14; matrix products, arithmetic and copies ran while one was open for 13% -> 9% of each run, Pallas kernels for 0% -> 2%
where the time goes in v1:
time: 822 us; the launch traced here: 812 us
  waiting for transfers between devices  532 us (65%)
  matrix products  129 us (16%)
  starting transfers between devices  61.6 us (7%)
  Pallas kernels  52.1 us (6%)
  local copies, waits for them, and re-layouts  17.6 us (2%)
  between operations  15 us (2%)
    reduce_scatter x4, waiting for transfers between devices, scatter(): lax.psum_scatter(part, ('row', 'col'), scatter_dimension=0, tiled=True)  263 us
    all_gather x4, waiting for transfers between devices, gather(): return lax.all_gather(part, ('row', 'col'), axis=0, tiled=True)  214 us
    ppermute x8, waiting for transfers between devices, edges_of(): out.append(lax.ppermute(head, axis, [(i + 1, i) for i in range(count - 1)]))  53.4 us
    ppermute x8, starting transfers between devices, edges_of(): out.append(lax.ppermute(tail, axis, [(i, i + 1) for i in range(count - 1)]))  50.6 us
    dot_general x4, matrix products, per_device(): left = jnp.einsum('wkr,rc->kwc', r, masked, precision=high)  39.3 us
    dot_general x4, matrix products, per_device(): jnp.einsum('wkr,kwc->rc', r, c, precision=high)  36.9 us
    pallas_call x2, Pallas kernels, primal_step(): pl.pallas_call(primal_kernel, grid=(steps,), in_specs=[whole] * 6 + halo,...  33.3 us
    dot_general x4, matrix products, per_device(): fields = scatter(jnp.einsum('kwc,wzc->kwz', left, c, precision=high))  28.6 us
  transfers between devices with their start and end apart: 26, of which 14 were waited for; matrix products, arithmetic and copies ran while one was open for 9% of the time, Pallas kernels for 2%

profile of v1, /device:TPU:0, one launch (start us, length us, event | category | flops | bytes accessed | tf_op | source)
XLA Modules:
  0.0 812.2 jit_solution(8201929676662335505)
XLA Ops:
  11.0 62.8 %all-gather.7.cloned.1.call-done = f32[512,2,512]{2,0,1:T(8,128)} async-done(((f32[32,2,512]{2,0,1:T(8,128)}), f32[512,2,512]{2,0,1:T(8,128)}) %all-gather.7.cloned.1.call-update) | async-done | bytes 2097168 | tf_op jit(solution)/shard_map/all_gather | solution.py:104
  88.2 48.0 %all-gather.5.cloned.1.call-done = f32[512,2,512]{2,0,1:T(8,128)} async-done(((f32[32,2,512]{2,0,1:T(8,128)}), f32[512,2,512]{2,0,1:T(8,128)}) %all-gather.5.cloned.1.call-update) | async-done | bytes 2097168 | tf_op jit(solution)/shard_map/all_gather | solution.py:104
  167.4 10.8 %collective-permute-done.4.right = f32[1024,1]{1,0:T(8,128)S(1)} collective-permute-done((f32[1024,1]{1,0:T(8,128)S(1)}, f32[1024,1]{1,0:T(8,128)S(1)}, u32[]{:S(2)}, u32[]{:S(2)}) %collective-permute-start.4) | collective-permute-done | bytes 4128 | tf_op jit(solution)/shard_map/ppermute | solution.py:99
  179.1 16.6 %shard_map.103 = (f32[1024,1024]{1,0:T(8,128)}, f32[1024,1024]{1,0:T(8,128)}, f32[1024,1024]{1,0:T(8,128)}) custom-call(f32[1024,1024]{1,0:T(8,128)} %copy-done, f32[1024,1024]{1,0:T(8,128)} %collective-permute-done.other, f32[1024,1024]{1,0:T(8,128)} %primal.1, s32[1024,1024]{1,0:T(8,128)} %pupil_m.3, s32[1024,1024]{1,0:T(8,128)} %lyot_m.3, ...), custom_call_target="tpu_custom_call" | custom-call | flops 31457280 | bytes 37748736 | tf_op jit(solution)/shard_map/pallas_call | solution.py:69
  195.8 9.8 %fusion.11 = f32[1024,2,512]{0,2,1:T(8,128)S(1)} fusion(f32[1024,1024]{1,0:T(8,128)} %get-tuple-element.9, f32[4,512,1024]{2,1,0:T(8,128)} %param.14), kind=kOutput, calls=%fused_computation.12 | convolution fusion | flops 6442450944 | bytes 12582912 | tf_op jit(solution)/shard_map/wkr,rc->kwc/dot_general | solution.py:143
  212.8 9.8 %fusion.9 = f32[1024,2,512]{0,2,1:T(8,128)S(1)} fusion(f32[1024,1024]{1,0:T(8,128)} %get-tuple-element.9, f32[4,512,1024]{2,1,0:T(8,128)} %param.14), kind=kOutput, calls=%fused_computation.10 | convolution fusion | flops 6442450944 | bytes 12582912 | tf_op jit(solution)/shard_map/wkr,rc->kwc/dot_general | solution.py:143
  229.9 73.7 %reduce-scatter.5.cloned.1.call-done = f32[32,2,512]{2,0,1:T(8,128)} async-done(((f32[512,2,512]{2,0,1:T(8,128)}), f32[32,2,512]{2,0,1:T(8,128)}) %reduce-scatter.5.cloned.1.call-update) | async-done | bytes 131088 | tf_op jit(solution)/shard_map/reduce_scatter | solution.py:108
  303.6 80.5 %reduce-scatter.7.cloned.1.call-done = f32[32,2,512]{2,0,1:T(8,128)} async-done(((f32[512,2,512]{2,0,1:T(8,128)}), f32[32,2,512]{2,0,1:T(8,128)}) %reduce-scatter.7.cloned.1.call-update) | async-done | bytes 131088 | tf_op jit(solution)/shard_map/reduce_scatter | solution.py:108
  386.6 56.9 %all-gather.11.cloned.1.call-done = f32[512,2,512]{2,0,1:T(8,128)} async-done(((f32[32,2,512]{2,0,1:T(8,128)}), f32[512,2,512]{2,0,1:T(8,128)}) %all-gather.11.cloned.1.call-update) | async-done | bytes 2097168 | tf_op jit(solution)/shard_map/all_gather | solution.py:104
  449.4 9.8 %fusion.5 = f32[1024,1024,1]{0,1,2:T(8,128)} fusion(f32[2,512,1024]{1,2,0:T(8,128)S(1)} %fusion.24, f32[4,512,1024]{2,1,0:T(8,128)} %param.14), kind=kOutput, calls=%fused_computation.6 | convolution fusion | flops 6442450944 | bytes 12582912 | tf_op jit(solution)/shard_map/wkr,kwc->rc/dot_general | solution.py:136
  459.3 46.5 %all-gather.9.cloned.1.call-done = f32[512,2,512]{2,0,1:T(8,128)} async-done(((f32[32,2,512]{2,0,1:T(8,128)}), f32[512,2,512]{2,0,1:T(8,128)}) %all-gather.9.cloned.1.call-update) | async-done | bytes 2097168 | tf_op jit(solution)/shard_map/all_gather | solution.py:104
  512.0 10.2 %fusion.4.mine = f32[1024,1024]{1,0:T(8,128)} fusion(f32[1024,1024,1]{0,1,2:T(8,128)S(1)} %copy-done.23, f32[4,512,1024]{2,1,0:T(8,128)} %param.14, f32[2,512,1024]{1,2,0:T(8,128)S(1)} %fusion.36), kind=kOutput, calls=%fused_computation.5 | convolution fusion | flops 6443499520 | bytes 16777216 | tf_op jit(solution)/shard_map/wkr,kwc->rc/dot_general | solution.py:136
  536.3 10.5 %collective-permute-done.9.right = f32[1024,1]{1,0:T(8,128)S(1)} collective-permute-done((f32[1024,1]{1,0:T(8,128)S(1)}, f32[1024,1]{1,0:T(8,128)S(1)}, u32[]{:S(2)}, u32[]{:S(2)}) %collective-permute-start.9) | collective-permute-done | bytes 4128 | tf_op jit(solution)/shard_map/ppermute | solution.py:99
  548.4 9.4 %shard_map.104.dual.above.below = f32[1024,1024]{1,0:T(8,128)} custom-call(f32[1024,1024]{1,0:T(8,128)} %dual.3, f32[1024,1024]{1,0:T(8,128)} %get-tuple-element.11.ext.above.below, f32[1024,1024]{1,0:T(8,128)} %get-tuple-element.11.ext.above.below, f32[1024,1024]{1,0:T(8,128)} %get-tuple-element.11.ext.above.below, f32[1,1024]{1,0:T(1,128)} %copy-done.20, ...), custom_call_target="tpu_custom_call" | custom-call | flops 20971520 | bytes 12582912 | tf_op jit(solution)/shard_map/pallas_call | solution.py:82
  567.2 11.5 %collective-permute-start.12 = (f32[1024,1]{1,0:T(8,128)S(1)}, f32[1024,1]{1,0:T(8,128)S(1)}, u32[]{:S(2)}, u32[]{:S(2)}) collective-permute-start(f32[1024,1]{1,0:T(8,128)S(1)} %get-tuple-element.23), channel_id=1, source_target_pairs={{0,2},{2,4},{4,6},{1,3},{3,5},{5,7},{8,10},{10,12},{12,14},{9,11},... | collective-permute-start | bytes 12296 | tf_op jit(solution)/shard_map/ppermute | solution.py:98
  578.8 10.8 %collective-permute-done.13.right = f32[1024,1]{1,0:T(8,128)S(1)} collective-permute-done((f32[1024,1]{1,0:T(8,128)S(1)}, f32[1024,1]{1,0:T(8,128)S(1)}, u32[]{:S(2)}, u32[]{:S(2)}) %collective-permute-start.13) | collective-permute-done | bytes 4128 | tf_op jit(solution)/shard_map/ppermute | solution.py:99
  590.5 16.7 %shard_map.105 = (f32[1024,1024]{1,0:T(8,128)}, f32[1024,1024]{1,0:T(8,128)}, f32[1024,1024]{1,0:T(8,128)}) custom-call(f32[1024,1024]{1,0:T(8,128)} %fusion.4.mine, f32[1024,1024]{1,0:T(8,128)} %collective-permute-done.5.other, f32[1024,1024]{1,0:T(8,128)} %get-tuple-element.10.primal, s32[1024,1024]{1,0:T(8,128)} %pupil_m.3, s32[1024,1024]{1,0:T(8,128)} %lyot_m.3, ...), custom_call_target="tpu_custom_call" | custom-call | flops 31457280 | bytes 37748736 | tf_op jit(solution)/shard_map/pallas_call | solution.py:69
  607.2 9.8 %fusion.2 = f32[1024,2,512]{0,2,1:T(8,128)S(1)} fusion(f32[1024,1024]{1,0:T(8,128)} %get-tuple-element.13, f32[4,512,1024]{2,1,0:T(8,128)} %param.14), kind=kOutput, calls=%fused_computation.2 | convolution fusion | flops 6442450944 | bytes 12582912 | tf_op jit(solution)/shard_map/wkr,rc->kwc/dot_general | solution.py:143
  624.5 9.8 %fusion = f32[1024,2,512]{0,2,1:T(8,128)S(1)} fusion(f32[1024,1024]{1,0:T(8,128)} %get-tuple-element.13, f32[4,512,1024]{2,1,0:T(8,128)} %param.14), kind=kOutput, calls=%fused_computation | convolution fusion | flops 6442450944 | bytes 12582912 | tf_op jit(solution)/shard_map/wkr,rc->kwc/dot_general | solution.py:143
  650.8 11.1 %collective-permute-start.16 = (f32[1024,1]{1,0:T(8,128)S(1)}, f32[1024,1]{1,0:T(8,128)S(1)}, u32[]{:S(2)}, u32[]{:S(2)}) collective-permute-start(f32[1024,1]{1,0:T(8,128)S(1)} %get-tuple-element.19), channel_id=1, source_target_pairs={{0,2},{2,4},{4,6},{1,3},{3,5},{5,7},{8,10},{10,12},{12,14},{9,11},... | collective-permute-start | bytes 12296 | tf_op jit(solution)/shard_map/ppermute | solution.py:98
  662.0 21.4 %collective-permute-done.17.right = f32[1024,1]{1,0:T(8,128)S(1)} collective-permute-done((f32[1024,1]{1,0:T(8,128)S(1)}, f32[1024,1]{1,0:T(8,128)S(1)}, u32[]{:S(2)}, u32[]{:S(2)}) %collective-permute-start.17) | collective-permute-done | bytes 4128 | tf_op jit(solution)/shard_map/ppermute | solution.py:99
  685.0 9.4 %shard_map.106 = f32[1024,1024]{1,0:T(8,128)} custom-call(f32[1024,1024]{1,0:T(8,128)} %shard_map.104.dual.above.below, f32[1024,1024]{1,0:T(8,128)} %get-tuple-element.14.ext.above.below, f32[1024,1024]{1,0:T(8,128)} %get-tuple-element.14.ext.above.below, f32[1024,1024]{1,0:T(8,128)} %get-tuple-element.14.ext.above.below, f32[1,1024]{1,0:T(1,128)} %copy-done.19, ...), custom_call_target="tpu_custom_call" | custom-call | flops 20971520 | bytes 12582912 | tf_op jit(solution)/shard_map/pallas_call | solution.py:82
  694.4 25.9 %reduce-scatter.9.cloned.1.call-done = f32[32,2,512]{2,0,1:T(8,128)} async-done(((f32[512,2,512]{2,0,1:T(8,128)}), f32[32,2,512]{2,0,1:T(8,128)}) %reduce-scatter.9.cloned.1.call-update) | async-done | bytes 131088 | tf_op jit(solution)/shard_map/reduce_scatter | solution.py:108
  720.2 82.7 %reduce-scatter.11.cloned.1.call-done = f32[32,2,512]{2,0,1:T(8,128)} async-done(((f32[512,2,512]{2,0,1:T(8,128)}), f32[32,2,512]{2,0,1:T(8,128)}) %reduce-scatter.11.cloned.1.call-update) | async-done | bytes 131088 | tf_op jit(solution)/shard_map/reduce_scatter | solution.py:108
  (119 shorter events, 132.6 us)
Async XLA Ops:
  7.2 66.7 %all-gather.7.cloned.1.call-start = ((), (), s32[]{:S(2)}) async-start(), calls=%async_computation.5 | async-start | bytes 2228224 | tf_op jit(solution)/shard_map/all_gather | solution.py:104
  10.2 126.1 %all-gather.5.cloned.1.call-start = ((), (), s32[]{:S(2)}) async-start(), calls=%async_computation.4 | async-start | bytes 2228224 | tf_op jit(solution)/shard_map/all_gather | solution.py:104
  10.9 292.6 %reduce-scatter.5.cloned.1.call-start = ((), (), s32[]{:S(2)}) async-start(), calls=%async_computation.6 | async-start | bytes 2228224 | tf_op jit(solution)/shard_map/reduce_scatter | solution.py:108
  153.1 25.2 %collective-permute-start = (f32[1024,1024]{1,0:T(8,128)S(1)}, f32[1024,1024]{1,0:T(8,128)}, u32[]{:S(2)}, u32[]{:S(2)}) collective-permute-start(f32[1024,1024]{1,0:T(8,128)S(1)} %fusion.13.mine), channel_id=1, source_target_pairs={{0,1},{1,0},{2,3},{3,2},{4,5},{5,4},{6,7},{7,6},{8,9},{9,8},{10,11... | collective-permute-start | bytes 12582920 | tf_op jit(solution)/shard_map/ppermute | solution.py:116
  153.9 13.5 %collective-permute-start.2 = (f32[1,1024]{1,0:T(1,128)S(1)}, f32[1,1024]{1,0:T(1,128)S(1)}, u32[]{:S(2)}, u32[]{:S(2)}) collective-permute-start(f32[1,1024]{1,0:T(1,128)S(1)} %get-tuple-element.32), channel_id=1, source_target_pairs={{8,0},{16,8},{24,16},{9,1},{17,9},{25,17},{10,2},{18,10},{26,18},{... | collective-permute-start | bytes 12296 | tf_op jit(solution)/shard_map/ppermute | solution.py:99
  161.5 16.7 %collective-permute-start.4 = (f32[1024,1]{1,0:T(8,128)S(1)}, f32[1024,1]{1,0:T(8,128)S(1)}, u32[]{:S(2)}, u32[]{:S(2)}) collective-permute-start(f32[1024,1]{1,0:T(8,128)S(1)} %get-tuple-element.30), channel_id=1, source_target_pairs={{2,0},{4,2},{6,4},{3,1},{5,3},{7,5},{10,8},{12,10},{14,12},{11,9},... | collective-permute-start | bytes 12296 | tf_op jit(solution)/shard_map/ppermute | solution.py:99
  162.8 15.6 %collective-permute-start.3 = (f32[1024,1]{1,0:T(8,128)S(1)}, f32[1024,1]{1,0:T(8,128)S(1)}, u32[]{:S(2)}, u32[]{:S(2)}) collective-permute-start(f32[1024,1]{1,0:T(8,128)S(1)} %get-tuple-element.31), channel_id=1, source_target_pairs={{0,2},{2,4},{4,6},{1,3},{3,5},{5,7},{8,10},{10,12},{12,14},{9,11},... | collective-permute-start | bytes 12296 | tf_op jit(solution)/shard_map/ppermute | solution.py:98
  212.7 171.3 %reduce-scatter.7.cloned.1.call-start = ((), (), s32[]{:S(2)}) async-start(), calls=%async_computation.8 | async-start | bytes 2228224 | tf_op jit(solution)/shard_map/reduce_scatter | solution.py:108
  229.8 213.6 %all-gather.11.cloned.1.call-start = ((), (), s32[]{:S(2)}) async-start(), calls=%async_computation.9 | async-start | bytes 2228224 | tf_op jit(solution)/shard_map/all_gather | solution.py:104
  385.8 119.9 %all-gather.9.cloned.1.call-start = ((), (), s32[]{:S(2)}) async-start(), calls=%async_computation.7 | async-start | bytes 2228224 | tf_op jit(solution)/shard_map/all_gather | solution.py:104
  386.4 333.8 %reduce-scatter.9.cloned.1.call-start = ((), (), s32[]{:S(2)}) async-start(), calls=%async_computation.10 | async-start | bytes 2228224 | tf_op jit(solution)/shard_map/reduce_scatter | solution.py:108
  522.1 67.4 %collective-permute-start.5 = (f32[1024,1024]{1,0:T(8,128)}, f32[1024,1024]{1,0:T(8,128)}, u32[]{:S(2)}, u32[]{:S(2)}) collective-permute-start(f32[1024,1024]{1,0:T(8,128)} %fusion.4.mine), channel_id=1, source_target_pairs={{0,1},{1,0},{2,3},{3,2},{4,5},{5,4},{6,7},{7,6},{8,9},{9,8},{10,11... | collective-permute-start | bytes 12582920 | tf_op jit(solution)/shard_map/ppermute | solution.py:116
  522.9 13.4 %collective-permute-start.7 = (f32[1,1024]{1,0:T(1,128)S(1)}, f32[1,1024]{1,0:T(1,128)S(1)}, u32[]{:S(2)}, u32[]{:S(2)}) collective-permute-start(f32[1,1024]{1,0:T(1,128)S(1)} %get-tuple-element.28), channel_id=1, source_target_pairs={{8,0},{16,8},{24,16},{9,1},{17,9},{25,17},{10,2},{18,10},{26,18},{... | collective-permute-start | bytes 12296 | tf_op jit(solution)/shard_map/ppermute | solution.py:99
  530.2 16.7 %collective-permute-start.9 = (f32[1024,1]{1,0:T(8,128)S(1)}, f32[1024,1]{1,0:T(8,128)S(1)}, u32[]{:S(2)}, u32[]{:S(2)}) collective-permute-start(f32[1024,1]{1,0:T(8,128)S(1)} %get-tuple-element.26), channel_id=1, source_target_pairs={{2,0},{4,2},{6,4},{3,1},{5,3},{7,5},{10,8},{12,10},{14,12},{11,9},... | collective-permute-start | bytes 12296 | tf_op jit(solution)/shard_map/ppermute | solution.py:99
  531.5 15.6 %collective-permute-start.8 = (f32[1024,1]{1,0:T(8,128)S(1)}, f32[1024,1]{1,0:T(8,128)S(1)}, u32[]{:S(2)}, u32[]{:S(2)}) collective-permute-start(f32[1024,1]{1,0:T(8,128)S(1)} %get-tuple-element.27), channel_id=1, source_target_pairs={{0,2},{2,4},{4,6},{1,3},{3,5},{5,7},{8,10},{10,12},{12,14},{9,11},... | collective-permute-start | bytes 12296 | tf_op jit(solution)/shard_map/ppermute | solution.py:98
  558.6 20.1 %collective-permute-start.11 = (f32[1,1024]{1,0:T(1,128)S(1)}, f32[1,1024]{1,0:T(1,128)S(1)}, u32[]{:S(2)}, u32[]{:S(2)}) collective-permute-start(f32[1,1024]{1,0:T(1,128)S(1)} %get-tuple-element.24), channel_id=1, source_target_pairs={{8,0},{16,8},{24,16},{9,1},{17,9},{25,17},{10,2},{18,10},{26,18},{... | collective-permute-start | bytes 12296 | tf_op jit(solution)/shard_map/ppermute | solution.py:99
  559.9 18.8 %collective-permute-start.10 = (f32[1,1024]{1,0:T(1,128)S(1)}, f32[1,1024]{1,0:T(1,128)S(1)}, u32[]{:S(2)}, u32[]{:S(2)}) collective-permute-start(f32[1,1024]{1,0:T(1,128)S(1)} %get-tuple-element.25), channel_id=1, source_target_pairs={{0,8},{8,16},{16,24},{1,9},{9,17},{17,25},{2,10},{10,18},{18,26},{... | collective-permute-start | bytes 12296 | tf_op jit(solution)/shard_map/ppermute | solution.py:98
  565.9 23.7 %collective-permute-start.13 = (f32[1024,1]{1,0:T(8,128)S(1)}, f32[1024,1]{1,0:T(8,128)S(1)}, u32[]{:S(2)}, u32[]{:S(2)}) collective-permute-start(f32[1024,1]{1,0:T(8,128)S(1)} %get-tuple-element.22), channel_id=1, source_target_pairs={{2,0},{4,2},{6,4},{3,1},{5,3},{7,5},{10,8},{12,10},{14,12},{11,9},... | collective-permute-start | bytes 12296 | tf_op jit(solution)/shard_map/ppermute | solution.py:99
  567.2 22.4 %collective-permute-start.12 = (f32[1024,1]{1,0:T(8,128)S(1)}, f32[1024,1]{1,0:T(8,128)S(1)}, u32[]{:S(2)}, u32[]{:S(2)}) collective-permute-start(f32[1024,1]{1,0:T(8,128)S(1)} %get-tuple-element.23), channel_id=1, source_target_pairs={{0,2},{2,4},{4,6},{1,3},{3,5},{5,7},{8,10},{10,12},{12,14},{9,11},... | collective-permute-start | bytes 12296 | tf_op jit(solution)/shard_map/ppermute | solution.py:98
  624.2 178.8 %reduce-scatter.11.cloned.1.call-start = ((), (), s32[]{:S(2)}) async-start(), calls=%async_computation.11 | async-start | bytes 2228224 | tf_op jit(solution)/shard_map/reduce_scatter | solution.py:108
  642.3 19.7 %collective-permute-start.15 = (f32[1,1024]{1,0:T(1,128)S(1)}, f32[1,1024]{1,0:T(1,128)S(1)}, u32[]{:S(2)}, u32[]{:S(2)}) collective-permute-start(f32[1,1024]{1,0:T(1,128)S(1)} %get-tuple-element.20), channel_id=1, source_target_pairs={{8,0},{16,8},{24,16},{9,1},{17,9},{25,17},{10,2},{18,10},{26,18},{... | collective-permute-start | bytes 12296 | tf_op jit(solution)/shard_map/ppermute | solution.py:99
  643.5 18.5 %collective-permute-start.14 = (f32[1,1024]{1,0:T(1,128)S(1)}, f32[1,1024]{1,0:T(1,128)S(1)}, u32[]{:S(2)}, u32[]{:S(2)}) collective-permute-start(f32[1,1024]{1,0:T(1,128)S(1)} %get-tuple-element.21), channel_id=1, source_target_pairs={{0,8},{8,16},{16,24},{1,9},{9,17},{17,25},{2,10},{10,18},{18,26},{... | collective-permute-start | bytes 12296 | tf_op jit(solution)/shard_map/ppermute | solution.py:98
  649.5 33.9 %collective-permute-start.17 = (f32[1024,1]{1,0:T(8,128)S(1)}, f32[1024,1]{1,0:T(8,128)S(1)}, u32[]{:S(2)}, u32[]{:S(2)}) collective-permute-start(f32[1024,1]{1,0:T(8,128)S(1)} %get-tuple-element.18), channel_id=1, source_target_pairs={{2,0},{4,2},{6,4},{3,1},{5,3},{7,5},{10,8},{12,10},{14,12},{11,9},... | collective-permute-start | bytes 12296 | tf_op jit(solution)/shard_map/ppermute | solution.py:99
  650.8 32.6 %collective-permute-start.16 = (f32[1024,1]{1,0:T(8,128)S(1)}, f32[1024,1]{1,0:T(8,128)S(1)}, u32[]{:S(2)}, u32[]{:S(2)}) collective-permute-start(f32[1024,1]{1,0:T(8,128)S(1)} %get-tuple-element.19), channel_id=1, source_target_pairs={{0,2},{2,4},{4,6},{1,3},{3,5},{5,7},{8,10},{10,12},{12,14},{9,11},... | collective-permute-start | bytes 12296 | tf_op jit(solution)/shard_map/ppermute | solution.py:98
  (26 other events, 786.3 us)
Sparse Core Ops, SparseCore 0:
  10.7 63.0 all-gather.6
  77.1 59.0 all-gather.4
  212.8 90.6 reduce-scatter.4
  305.7 78.2 reduce-scatter.6
  386.7 56.7 all-gather.10
  446.7 59.0 all-gather.8
  624.3 95.9 reduce-scatter.8
  722.5 80.3 reduce-scatter.10

commit v2 on v1

--- a/solution.py
+++ b/solution.py
@@ -13,7 +13,7 @@
 contrast = 0.5
 curvature_limit = 0.1
 high = lax.Precision.HIGH
-CHUNKS = 2
+CHUNKS = 1
 
 
 def around(v, above8, below8, top, bottom, left, right):
@@ -130,7 +130,9 @@
     primal, dual_c = transmission, dual_curvature
     fulls = [gather(d) for d in duals]
     for iteration in range(ITERS):
-        dual_edges = edges_of(dual_c)
+        if iteration == 0:
+            dual_edges = edges_of(dual_c)
+            fulls, dual_edges = lax.optimization_barrier((fulls, dual_edges))
         carried = [jnp.einsum("kwz,wzc->kwc", f, c, precision=high) for f, c in zip(fulls, cols_of)]
         backward = functools.reduce(
             jnp.add, [jnp.einsum("wkr,kwc->rc", r, c, precision=high) for r, c in zip(rows_of, carried)]
@@ -139,16 +141,21 @@
         primal, extended, masked = primal_step(backward, other, primal, pupil_mask, lyot_mask, dual_c, dual_edges)
         new_duals = []
         fulls = []
-        for r, c, d, k in zip(rows_of, cols_of, duals, darks):
+        summed = []
+        for r, c in zip(rows_of, cols_of):
             left = jnp.einsum("wkr,rc->kwc", r, masked, precision=high)
-            fields = scatter(jnp.einsum("kwc,wzc->kwz", left, c, precision=high))
+            summed.append(scatter(jnp.einsum("kwc,wzc->kwz", left, c, precision=high)))
+        dual_c = dual_step(dual_c, extended, edges_of(extended))
+        if iteration < ITERS - 1:
+            dual_edges = edges_of(dual_c)
+            summed, dual_c, dual_edges = lax.optimization_barrier((summed, dual_c, dual_edges))
+        for fields, d, k in zip(summed, duals, darks):
             shifted = d + step_dual * fields
             new = k * (shifted - step_dual * jnp.clip(shifted / step_dual, -contrast, contrast))
             new_duals.append(new)
             if iteration < ITERS - 1:
                 fulls.append(gather(new))
         duals = new_duals
-        dual_c = dual_step(dual_c, extended, edges_of(extended))
     return (primal, jnp.concatenate(duals, axis=1), dual_c)
 
 

time: 822 us -> 605 us (0.74)
  waiting for transfers between devices: 532 us -> 335 us
  matrix products: 129 us -> 107 us
    reduce_scatter x4 -> x2, waiting for transfers between devices: 263 us -> 99.7 us  [scatter(): lax.psum_scatter(part, ('row', 'col'), scatter_dimension=0, tiled=True)]
    all_gather x4 -> x2, waiting for transfers between devices: 214 us -> 135 us  [gather(): return lax.all_gather(part, ('row', 'col'), axis=0, tiled=True)]
    ppermute x8, waiting for transfers between devices: 53.4 us -> 78.4 us  [edges_of(): out.append(lax.ppermute(head, axis, [(i + 1, i) for i in range(count - 1)]))]
    ppermute x2, waiting for transfers between devices: 0.01 us -> 14.4 us  [other_waves(): return lax.ppermute(part, 'wave', [(0, 1), (1, 0)])]
    dot_general x4 -> x2, matrix products: 28.6 us -> 21.2 us  [per_device(): summed.append(scatter(jnp.einsum('kwc,wzc->kwz', left, c, precision=high)))]
    dot_general x4 -> x2, matrix products: 36.9 us -> 31.6 us  [per_device(): jnp.einsum('wkr,kwc->rc', r, c, precision=high)]
    dot_general x4 -> x2, matrix products: 39.3 us -> 34 us  [per_device(): left = jnp.einsum('wkr,rc->kwc', r, masked, precision=high)]
    dot_general x4 -> x2, matrix products: 24.3 us -> 20.3 us  [per_device(): jnp.einsum('kwz,wzc->kwc', f, c, precision=high)]
  transfers between devices with their start and end apart: 26 -> 22, of which waited for: 14 -> 12; matrix products, arithmetic and copies ran while one was open for 9% -> 1% of each run, Pallas kernels for 2% -> 3%
where the time goes in v2:
time: 605 us; the launch traced here: 595 us
  waiting for transfers between devices  335 us (55%)
  matrix products  107 us (18%)
  starting transfers between devices  64 us (11%)
  Pallas kernels  52.1 us (9%)
  local copies, waits for them, and re-layouts  17.3 us (3%)
  between operations  14.6 us (2%)
    all_gather x2, waiting for transfers between devices, gather(): return lax.all_gather(part, ('row', 'col'), axis=0, tiled=True)  135 us
    reduce_scatter x2, waiting for transfers between devices, scatter(): lax.psum_scatter(part, ('row', 'col'), scatter_dimension=0, tiled=True)  99.7 us
    ppermute x8, waiting for transfers between devices, edges_of(): out.append(lax.ppermute(head, axis, [(i + 1, i) for i in range(count - 1)]))  78.4 us
    ppermute x8, starting transfers between devices, edges_of(): out.append(lax.ppermute(tail, axis, [(i, i + 1) for i in range(count - 1)]))  53.5 us
    dot_general x2, matrix products, per_device(): left = jnp.einsum('wkr,rc->kwc', r, masked, precision=high)  34 us
    pallas_call x2, Pallas kernels, primal_step(): pl.pallas_call(primal_kernel, grid=(steps,), in_specs=[whole] * 6 + halo,...  33.2 us
    dot_general x2, matrix products, per_device(): jnp.einsum('wkr,kwc->rc', r, c, precision=high)  31.6 us
    dot_general x2, matrix products, per_device(): summed.append(scatter(jnp.einsum('kwc,wzc->kwz', left, c, precision=high)))  21.2 us
  transfers between devices with their start and end apart: 22, of which 12 were waited for; matrix products, arithmetic and copies ran while one was open for 1% of the time, Pallas kernels for 3%

profile of v2, /device:TPU:0, one launch (start us, length us, event | category | flops | bytes accessed | tf_op | source)
XLA Modules:
  0.0 595.2 jit_solution(16108363923669064788)
XLA Ops:
  11.2 5.6 collective-permute-start
  24.2 12.7 %collective-permute-done.3.right = f32[1024,1]{1,0:T(8,128)S(1)} collective-permute-done((f32[1024,1]{1,0:T(8,128)S(1)}, f32[1024,1]{1,0:T(8,128)S(1)}, u32[]{:S(2)}, u32[]{:S(2)}) %collective-permute-start.3) | collective-permute-done | bytes 4128 | tf_op jit(solution)/shard_map/ppermute | solution.py:99
  36.9 58.0 %all-gather.3.cloned.1.call-done = f32[512,4,512]{2,0,1:T(8,128)} async-done(((f32[32,4,512]{2,0,1:T(8,128)}), f32[512,4,512]{2,0,1:T(8,128)}) %all-gather.3.cloned.1.call-update) | async-done | bytes 4194320 | tf_op jit(solution)/shard_map/all_gather | solution.py:104
  94.9 10.1 %fusion.22 = f32[4,512,1024]{1,2,0:T(8,128)S(1)} fusion(f32[512,4,512]{2,0,1:T(8,128)} %all-gather.3.cloned.1.call-done, f32[4,512,1024]{2,1,0:T(8,128)} %param.15), kind=kOutput, calls=%fused_computation.24 | convolution fusion | flops 6442450944 | bytes 20971520 | tf_op jit(solution)/shard_map/kwz,wzc->kwc/dot_general | solution.py:136
  105.0 15.8 %fusion.8.mine = f32[1024,1024]{1,0:T(8,128)S(1)} fusion(f32[4,512,1024]{2,1,0:T(8,128)} %param.14, f32[4,512,1024]{1,2,0:T(8,128)S(1)} %fusion.22), kind=kOutput, calls=%fused_computation.8 | convolution fusion | flops 12884901888 | bytes 20971520 | tf_op jit(solution)/shard_map/wkr,kwc->rc/dot_general | solution.py:138
  122.8 7.3 %collective-permute-done.4.other = f32[1024,1024]{1,0:T(8,128)} collective-permute-done((f32[1024,1024]{1,0:T(8,128)S(1)}, f32[1024,1024]{1,0:T(8,128)}, u32[]{:S(2)}, u32[]{:S(2)}) %collective-permute-start.4) | collective-permute-done | bytes 4194336 | tf_op jit(solution)/shard_map/ppermute | solution.py:116
  130.1 16.6 %shard_map.103 = (f32[1024,1024]{1,0:T(8,128)}, f32[1024,1024]{1,0:T(8,128)}, f32[1024,1024]{1,0:T(8,128)}) custom-call(f32[1024,1024]{1,0:T(8,128)} %copy-done.1, f32[1024,1024]{1,0:T(8,128)} %collective-permute-done.4.other, f32[1024,1024]{1,0:T(8,128)} %primal.1, s32[1024,1024]{1,0:T(8,128)} %pupil_m.3, s32[1024,1024]{1,0:T(8,128)} %lyot_m.3, ...), custom_call_target="tpu_custom_call" | custom-call | flops 31457280 | bytes 37748736 | tf_op jit(solution)/shard_map/pallas_call | solution.py:69
  146.7 17.0 %fusion.6 = f32[1024,4,512]{0,2,1:T(8,128)S(1)} fusion(f32[4,512,1024]{2,1,0:T(8,128)} %param.14, f32[1024,1024]{1,0:T(8,128)} %get-tuple-element.25), kind=kOutput, calls=%fused_computation.6 | convolution fusion | flops 12884901888 | bytes 20971520 | tf_op jit(solution)/shard_map/wkr,rc->kwc/dot_general | solution.py:146
  163.7 10.6 %convolution_bitcast_fusion.1 = f32[512,4,512]{2,0,1:T(8,128)} fusion(f32[1024,4,512]{0,2,1:T(8,128)S(1)} %fusion.6, f32[4,512,1024]{2,1,0:T(8,128)} %param.15), kind=kOutput, calls=%fused_computation.11 | convolution fusion | flops 6442450944 | bytes 20971520 | tf_op jit(solution)/shard_map/kwc,wzc->kwz/dot_general | solution.py:147
  188.4 21.8 %collective-permute-done.8.right = f32[1024,1]{1,0:T(8,128)S(1)} collective-permute-done((f32[1024,1]{1,0:T(8,128)S(1)}, f32[1024,1]{1,0:T(8,128)S(1)}, u32[]{:S(2)}, u32[]{:S(2)}) %collective-permute-start.8) | collective-permute-done | bytes 4128 | tf_op jit(solution)/shard_map/ppermute | solution.py:99
  214.9 9.4 %shard_map.104.dual.above.below = f32[1024,1024]{1,0:T(8,128)} custom-call(f32[1024,1024]{1,0:T(8,128)} %dual.3, f32[1024,1024]{1,0:T(8,128)} %get-tuple-element.26.ext.above.below, f32[1024,1024]{1,0:T(8,128)} %get-tuple-element.26.ext.above.below, f32[1024,1024]{1,0:T(8,128)} %get-tuple-element.26.ext.above.below, f32[1,1024]{1,0:T(1,128)} %copy-done.21, ...), custom_call_target="tpu_custom_call" | custom-call | flops 20971520 | bytes 12582912 | tf_op jit(solution)/shard_map/pallas_call | solution.py:82
  233.6 20.3 %collective-permute-start.11 = (f32[1024,1]{1,0:T(8,128)S(1)}, f32[1024,1]{1,0:T(8,128)S(1)}, u32[]{:S(2)}, u32[]{:S(2)}) collective-permute-start(f32[1024,1]{1,0:T(8,128)S(1)} %get-tuple-element.45), channel_id=1, source_target_pairs={{0,2},{2,4},{4,6},{1,3},{3,5},{5,7},{8,10},{10,12},{12,14},{9,11},... | collective-permute-start | bytes 12296 | tf_op jit(solution)/shard_map/ppermute | solution.py:98
  254.0 22.0 %collective-permute-done.12.right = f32[1024,1]{1,0:T(8,128)S(1)} collective-permute-done((f32[1024,1]{1,0:T(8,128)S(1)}, f32[1024,1]{1,0:T(8,128)S(1)}, u32[]{:S(2)}, u32[]{:S(2)}) %collective-permute-start.12) | collective-permute-done | bytes 4128 | tf_op jit(solution)/shard_map/ppermute | solution.py:99
  276.0 35.3 %reduce-scatter.3.cloned.1.call-done = f32[32,4,512]{2,0,1:T(8,128)} async-done(((f32[512,4,512]{2,0,1:T(8,128)}), f32[32,4,512]{2,0,1:T(8,128)}) %reduce-scatter.3.cloned.1.call-update) | async-done | bytes 262160 | tf_op jit(solution)/shard_map/reduce_scatter | solution.py:108
  313.3 76.8 %all-gather.5.cloned.1.call-done = f32[512,4,512]{2,0,1:T(8,128)} async-done(((f32[32,4,512]{2,0,1:T(8,128)}), f32[512,4,512]{2,0,1:T(8,128)}) %all-gather.5.cloned.1.call-update) | async-done | bytes 4194320 | tf_op jit(solution)/shard_map/all_gather | solution.py:104
  390.0 10.3 %fusion.23 = f32[4,512,1024]{1,2,0:T(8,128)S(1)} fusion(f32[512,4,512]{2,0,1:T(8,128)} %all-gather.5.cloned.1.call-done, f32[4,512,1024]{2,1,0:T(8,128)} %param.15), kind=kOutput, calls=%fused_computation.25 | convolution fusion | flops 6442450944 | bytes 20971520 | tf_op jit(solution)/shard_map/kwz,wzc->kwc/dot_general | solution.py:136
  400.3 15.8 %fusion.11.mine = f32[1024,1024]{1,0:T(8,128)S(1)} fusion(f32[4,512,1024]{2,1,0:T(8,128)} %param.14, f32[4,512,1024]{1,2,0:T(8,128)S(1)} %fusion.23), kind=kOutput, calls=%fused_computation.9 | convolution fusion | flops 12884901888 | bytes 20971520 | tf_op jit(solution)/shard_map/wkr,kwc->rc/dot_general | solution.py:138
  418.2 7.2 %collective-permute-done.13.other = f32[1024,1024]{1,0:T(8,128)S(1)} collective-permute-done((f32[1024,1024]{1,0:T(8,128)S(1)}, f32[1024,1024]{1,0:T(8,128)S(1)}, u32[]{:S(2)}, u32[]{:S(2)}) %collective-permute-start.13) | collective-permute-done | bytes 4194336 | tf_op jit(solution)/shard_map/ppermute | solution.py:116
  427.3 16.7 %shard_map.105 = (f32[1024,1024]{1,0:T(8,128)}, f32[1024,1024]{1,0:T(8,128)}, f32[1024,1024]{1,0:T(8,128)}) custom-call(f32[1024,1024]{1,0:T(8,128)} %copy-done, f32[1024,1024]{1,0:T(8,128)} %copy-done.2, f32[1024,1024]{1,0:T(8,128)} %get-tuple-element.28.primal, s32[1024,1024]{1,0:T(8,128)} %pupil_m.3, s32[1024,1024]{1,0:T(8,128)} %lyot_m.3, ...), custom_call_target="tpu_custom_call" | custom-call | flops 31457280 | bytes 37748736 | tf_op jit(solution)/shard_map/pallas_call | solution.py:69
  444.0 17.1 %fusion.4 = f32[1024,4,512]{0,2,1:T(8,128)S(1)} fusion(f32[4,512,1024]{2,1,0:T(8,128)} %param.14, f32[1024,1024]{1,0:T(8,128)} %get-tuple-element.35), kind=kOutput, calls=%fused_computation.4 | convolution fusion | flops 12884901888 | bytes 20971520 | tf_op jit(solution)/shard_map/wkr,rc->kwc/dot_general | solution.py:146
  461.0 10.6 %convolution_bitcast_fusion = f32[512,4,512]{2,0,1:T(8,128)} fusion(f32[1024,4,512]{0,2,1:T(8,128)S(1)} %fusion.4, f32[4,512,1024]{2,1,0:T(8,128)} %param.15), kind=kOutput, calls=%fused_computation.10 | convolution fusion | flops 6442450944 | bytes 20971520 | tf_op jit(solution)/shard_map/kwc,wzc->kwz/dot_general | solution.py:147
  485.8 21.8 %collective-permute-done.17.right = f32[1024,1]{1,0:T(8,128)S(1)} collective-permute-done((f32[1024,1]{1,0:T(8,128)S(1)}, f32[1024,1]{1,0:T(8,128)S(1)}, u32[]{:S(2)}, u32[]{:S(2)}) %collective-permute-start.17) | collective-permute-done | bytes 4128 | tf_op jit(solution)/shard_map/ppermute | solution.py:99
  512.4 9.5 %shard_map.106 = f32[1024,1024]{1,0:T(8,128)} custom-call(f32[1024,1024]{1,0:T(8,128)} %shard_map.104.dual.above.below, f32[1024,1024]{1,0:T(8,128)} %get-tuple-element.36.ext.above.below, f32[1024,1024]{1,0:T(8,128)} %get-tuple-element.36.ext.above.below, f32[1024,1024]{1,0:T(8,128)} %get-tuple-element.36.ext.above.below, f32[1,1024]{1,0:T(1,128)} %copy-done.20, ...), custom_call_target="tpu_custom_call" | custom-call | flops 20971520 | bytes 12582912 | tf_op jit(solution)/shard_map/pallas_call | solution.py:82
  521.8 64.4 %reduce-scatter.5.cloned.1.call-done = f32[32,4,512]{2,0,1:T(8,128)} async-done(((f32[512,4,512]{2,0,1:T(8,128)}), f32[32,4,512]{2,0,1:T(8,128)}) %reduce-scatter.5.cloned.1.call-update) | async-done | bytes 262160 | tf_op jit(solution)/shard_map/reduce_scatter | solution.py:108
  (92 shorter events, 68.1 us)
Async XLA Ops:
  7.2 87.7 %all-gather.3.cloned.1.call-start = ((), (), s32[]{:S(2)}) async-start(), calls=%async_computation.2 | async-start | bytes 4456448 | tf_op jit(solution)/shard_map/all_gather | solution.py:104
  9.1 302.2 %reduce-scatter.3.cloned.1.call-start = ((), (), s32[]{:S(2)}) async-start(), calls=%async_computation.3 | async-start | bytes 4456448 | tf_op jit(solution)/shard_map/reduce_scatter | solution.py:108
  10.0 14.2 %collective-permute-start.1 = (f32[1,1024]{1,0:T(1,128)S(1)}, f32[1,1024]{1,0:T(1,128)S(1)}, u32[]{:S(2)}, u32[]{:S(2)}) collective-permute-start(f32[1,1024]{1,0:T(1,128)S(1)} %get-tuple-element.54), channel_id=1, source_target_pairs={{8,0},{16,8},{24,16},{9,1},{17,9},{25,17},{10,2},{18,10},{26,18},{... | collective-permute-start | bytes 12296 | tf_op jit(solution)/shard_map/ppermute | solution.py:99
  11.2 12.9 %collective-permute-start = (f32[1,1024]{1,0:T(1,128)S(1)}, f32[1,1024]{1,0:T(1,128)S(1)}, u32[]{:S(2)}, u32[]{:S(2)}) collective-permute-start(f32[1,1024]{1,0:T(1,128)S(1)} %get-tuple-element.55), channel_id=1, source_target_pairs={{0,8},{8,16},{16,24},{1,9},{9,17},{17,25},{2,10},{10,18},{18,26},{... | collective-permute-start | bytes 12296 | tf_op jit(solution)/shard_map/ppermute | solution.py:98
  18.3 18.6 %collective-permute-start.3 = (f32[1024,1]{1,0:T(8,128)S(1)}, f32[1024,1]{1,0:T(8,128)S(1)}, u32[]{:S(2)}, u32[]{:S(2)}) collective-permute-start(f32[1024,1]{1,0:T(8,128)S(1)} %get-tuple-element.52), channel_id=1, source_target_pairs={{2,0},{4,2},{6,4},{3,1},{5,3},{7,5},{10,8},{12,10},{14,12},{11,9},... | collective-permute-start | bytes 12296 | tf_op jit(solution)/shard_map/ppermute | solution.py:99
  19.5 17.3 %collective-permute-start.2 = (f32[1024,1]{1,0:T(8,128)S(1)}, f32[1024,1]{1,0:T(8,128)S(1)}, u32[]{:S(2)}, u32[]{:S(2)}) collective-permute-start(f32[1024,1]{1,0:T(8,128)S(1)} %get-tuple-element.53), channel_id=1, source_target_pairs={{0,2},{2,4},{4,6},{1,3},{3,5},{5,7},{8,10},{10,12},{12,14},{9,11},... | collective-permute-start | bytes 12296 | tf_op jit(solution)/shard_map/ppermute | solution.py:98
  122.8 7.3 %collective-permute-start.4 = (f32[1024,1024]{1,0:T(8,128)S(1)}, f32[1024,1024]{1,0:T(8,128)}, u32[]{:S(2)}, u32[]{:S(2)}) collective-permute-start(f32[1024,1024]{1,0:T(8,128)S(1)} %fusion.8.mine), channel_id=1, source_target_pairs={{0,1},{1,0},{2,3},{3,2},{4,5},{5,4},{6,7},{7,6},{8,9},{9,8},{10,11... | collective-permute-start | bytes 12582920 | tf_op jit(solution)/shard_map/ppermute | solution.py:116
  174.2 215.8 %all-gather.5.cloned.1.call-start = ((), (), s32[]{:S(2)}) async-start(), calls=%async_computation.4 | async-start | bytes 4456448 | tf_op jit(solution)/shard_map/all_gather | solution.py:104
  175.1 13.3 %collective-permute-start.6 = (f32[1,1024]{1,0:T(1,128)S(1)}, f32[1,1024]{1,0:T(1,128)S(1)}, u32[]{:S(2)}, u32[]{:S(2)}) collective-permute-start(f32[1,1024]{1,0:T(1,128)S(1)} %get-tuple-element.50), channel_id=1, source_target_pairs={{8,0},{16,8},{24,16},{9,1},{17,9},{25,17},{10,2},{18,10},{26,18},{... | collective-permute-start | bytes 12296 | tf_op jit(solution)/shard_map/ppermute | solution.py:99
  176.4 12.0 %collective-permute-start.5 = (f32[1,1024]{1,0:T(1,128)S(1)}, f32[1,1024]{1,0:T(1,128)S(1)}, u32[]{:S(2)}, u32[]{:S(2)}) collective-permute-start(f32[1,1024]{1,0:T(1,128)S(1)} %get-tuple-element.51), channel_id=1, source_target_pairs={{0,8},{8,16},{16,24},{1,9},{9,17},{17,25},{2,10},{10,18},{18,26},{... | collective-permute-start | bytes 12296 | tf_op jit(solution)/shard_map/ppermute | solution.py:98
  182.3 27.9 %collective-permute-start.8 = (f32[1024,1]{1,0:T(8,128)S(1)}, f32[1024,1]{1,0:T(8,128)S(1)}, u32[]{:S(2)}, u32[]{:S(2)}) collective-permute-start(f32[1024,1]{1,0:T(8,128)S(1)} %get-tuple-element.48), channel_id=1, source_target_pairs={{2,0},{4,2},{6,4},{3,1},{5,3},{7,5},{10,8},{12,10},{14,12},{11,9},... | collective-permute-start | bytes 12296 | tf_op jit(solution)/shard_map/ppermute | solution.py:99
  183.6 30.5 %collective-permute-start.7 = (f32[1024,1]{1,0:T(8,128)S(1)}, f32[1024,1]{1,0:T(8,128)S(1)}, u32[]{:S(2)}, u32[]{:S(2)}) collective-permute-start(f32[1024,1]{1,0:T(8,128)S(1)} %get-tuple-element.49), channel_id=1, source_target_pairs={{0,2},{2,4},{4,6},{1,3},{3,5},{5,7},{8,10},{10,12},{12,14},{9,11},... | collective-permute-start | bytes 12296 | tf_op jit(solution)/shard_map/ppermute | solution.py:98
  225.1 28.9 %collective-permute-start.10 = (f32[1,1024]{1,0:T(1,128)S(1)}, f32[1,1024]{1,0:T(1,128)S(1)}, u32[]{:S(2)}, u32[]{:S(2)}) collective-permute-start(f32[1,1024]{1,0:T(1,128)S(1)} %get-tuple-element.46), channel_id=1, source_target_pairs={{8,0},{16,8},{24,16},{9,1},{17,9},{25,17},{10,2},{18,10},{26,18},{... | collective-permute-start | bytes 12296 | tf_op jit(solution)/shard_map/ppermute | solution.py:99
  226.4 27.6 %collective-permute-start.9 = (f32[1,1024]{1,0:T(1,128)S(1)}, f32[1,1024]{1,0:T(1,128)S(1)}, u32[]{:S(2)}, u32[]{:S(2)}) collective-permute-start(f32[1,1024]{1,0:T(1,128)S(1)} %get-tuple-element.47), channel_id=1, source_target_pairs={{0,8},{8,16},{16,24},{1,9},{9,17},{17,25},{2,10},{10,18},{18,26},{... | collective-permute-start | bytes 12296 | tf_op jit(solution)/shard_map/ppermute | solution.py:98
  232.3 43.7 %collective-permute-start.12 = (f32[1024,1]{1,0:T(8,128)S(1)}, f32[1024,1]{1,0:T(8,128)S(1)}, u32[]{:S(2)}, u32[]{:S(2)}) collective-permute-start(f32[1024,1]{1,0:T(8,128)S(1)} %get-tuple-element.44), channel_id=1, source_target_pairs={{2,0},{4,2},{6,4},{3,1},{5,3},{7,5},{10,8},{12,10},{14,12},{11,9},... | collective-permute-start | bytes 12296 | tf_op jit(solution)/shard_map/ppermute | solution.py:99
  233.6 42.4 %collective-permute-start.11 = (f32[1024,1]{1,0:T(8,128)S(1)}, f32[1024,1]{1,0:T(8,128)S(1)}, u32[]{:S(2)}, u32[]{:S(2)}) collective-permute-start(f32[1024,1]{1,0:T(8,128)S(1)} %get-tuple-element.45), channel_id=1, source_target_pairs={{0,2},{2,4},{4,6},{1,3},{3,5},{5,7},{8,10},{10,12},{12,14},{9,11},... | collective-permute-start | bytes 12296 | tf_op jit(solution)/shard_map/ppermute | solution.py:98
  253.9 146.4 %copy-start.14 = (f32[1,1024]{1,0:T(1,128)}, f32[1,1024]{1,0:T(1,128)S(1)}, u32[]{:S(2)}) copy-start(f32[1,1024]{1,0:T(1,128)S(1)} %collective-permute-done.10.bottom) | copy-start | bytes 12292
  254.0 146.3 %copy-start.15 = (f32[1,1024]{1,0:T(1,128)}, f32[1,1024]{1,0:T(1,128)S(1)}, u32[]{:S(2)}) copy-start(f32[1,1024]{1,0:T(1,128)S(1)} %collective-permute-done.9.top) | copy-start | bytes 12292
  313.2 273.0 %reduce-scatter.5.cloned.1.call-start = ((), (), s32[]{:S(2)}) async-start(), calls=%async_computation.5 | async-start | bytes 4456448 | tf_op jit(solution)/shard_map/reduce_scatter | solution.py:108
  418.2 7.2 %collective-permute-start.13 = (f32[1024,1024]{1,0:T(8,128)S(1)}, f32[1024,1024]{1,0:T(8,128)S(1)}, u32[]{:S(2)}, u32[]{:S(2)}) collective-permute-start(f32[1024,1024]{1,0:T(8,128)S(1)} %fusion.11.mine), channel_id=1, source_target_pairs={{0,1},{1,0},{2,3},{3,2},{4,5},{5,4},{6,7},{7,6},{8,9},{9,8},{10,11... | collective-permute-start | bytes 12582920 | tf_op jit(solution)/shard_map/ppermute | solution.py:116
  472.5 13.3 %collective-permute-start.15 = (f32[1,1024]{1,0:T(1,128)S(1)}, f32[1,1024]{1,0:T(1,128)S(1)}, u32[]{:S(2)}, u32[]{:S(2)}) collective-permute-start(f32[1,1024]{1,0:T(1,128)S(1)} %get-tuple-element.42), channel_id=1, source_target_pairs={{8,0},{16,8},{24,16},{9,1},{17,9},{25,17},{10,2},{18,10},{26,18},{... | collective-permute-start | bytes 12296 | tf_op jit(solution)/shard_map/ppermute | solution.py:99
  473.7 12.0 %collective-permute-start.14 = (f32[1,1024]{1,0:T(1,128)S(1)}, f32[1,1024]{1,0:T(1,128)S(1)}, u32[]{:S(2)}, u32[]{:S(2)}) collective-permute-start(f32[1,1024]{1,0:T(1,128)S(1)} %get-tuple-element.43), channel_id=1, source_target_pairs={{0,8},{8,16},{16,24},{1,9},{9,17},{17,25},{2,10},{10,18},{18,26},{... | collective-permute-start | bytes 12296 | tf_op jit(solution)/shard_map/ppermute | solution.py:98
  479.7 27.9 %collective-permute-start.17 = (f32[1024,1]{1,0:T(8,128)S(1)}, f32[1024,1]{1,0:T(8,128)S(1)}, u32[]{:S(2)}, u32[]{:S(2)}) collective-permute-start(f32[1024,1]{1,0:T(8,128)S(1)} %get-tuple-element.40), channel_id=1, source_target_pairs={{2,0},{4,2},{6,4},{3,1},{5,3},{7,5},{10,8},{12,10},{14,12},{11,9},... | collective-permute-start | bytes 12296 | tf_op jit(solution)/shard_map/ppermute | solution.py:99
  481.0 30.5 %collective-permute-start.16 = (f32[1024,1]{1,0:T(8,128)S(1)}, f32[1024,1]{1,0:T(8,128)S(1)}, u32[]{:S(2)}, u32[]{:S(2)}) collective-permute-start(f32[1024,1]{1,0:T(8,128)S(1)} %get-tuple-element.41), channel_id=1, source_target_pairs={{0,2},{2,4},{4,6},{1,3},{3,5},{5,7},{8,10},{10,12},{12,14},{9,11},... | collective-permute-start | bytes 12296 | tf_op jit(solution)/shard_map/ppermute | solution.py:98
  (20 other events, 1025.5 us)
Sparse Core Ops, SparseCore 0:
  11.3 83.5 all-gather.2
  174.4 136.9 reduce-scatter.2
  314.6 75.3 all-gather.4
  471.8 114.3 reduce-scatter.4

commit v3 on v2

--- a/solution.py
+++ b/solution.py
@@ -14,6 +14,7 @@
 curvature_limit = 0.1
 high = lax.Precision.HIGH
 CHUNKS = 1
+MESH = pl.DeviceIdType.MESH
 
 
 def around(v, above8, below8, top, bottom, left, right):
@@ -100,12 +101,113 @@
     return out
 
 
+def greet():
+    r, c, nr, nc = lax.axis_index("row"), lax.axis_index("col"), lax.axis_size("row"), lax.axis_size("col")
+    barrier = pltpu.get_barrier_semaphore()
+    for d in range(1, nr):
+        pl.semaphore_signal(barrier, inc=1, device_id={"row": lax.rem(r + d, nr)}, device_id_type=MESH)
+    for e in range(1, nc):
+        pl.semaphore_signal(barrier, inc=1, device_id={"col": lax.rem(c + e, nc)}, device_id_type=MESH)
+    pl.semaphore_wait(barrier, nr + nc - 2)
+    return r, c, nr, nc
+
+
+def gather_kernel(x_ref, out_ref, send_r, recv_r, send_c, recv_c):
+    r, c, nr, nc = greet()
+    mine = r * nc + c
+    sent = []
+    for d in range(1, nr):
+        copy = pltpu.make_async_remote_copy(
+            src_ref=x_ref, dst_ref=out_ref.at[mine], send_sem=send_r.at[d], recv_sem=recv_r.at[d],
+            device_id={"row": lax.rem(r + d, nr)}, device_id_type=MESH)
+        copy.start()
+        sent.append(copy)
+    along = list(sent)
+    across = []
+    for d in range(nr):
+        slot = lax.rem(r + nr - d, nr) * nc + c
+        if d > 0:
+            along[d - 1].wait_recv()
+        for e in range(1, nc):
+            copy = pltpu.make_async_remote_copy(
+                src_ref=x_ref if d == 0 else out_ref.at[slot], dst_ref=out_ref.at[slot],
+                send_sem=send_c.at[d * nc + e], recv_sem=recv_c.at[d * nc + e],
+                device_id={"col": lax.rem(c + e, nc)}, device_id_type=MESH)
+            copy.start()
+            across.append(copy)
+    out_ref[mine] = x_ref[...]
+    for copy in across:
+        copy.wait_recv()
+    for copy in along + across:
+        copy.wait_send()
+
+
+def scatter_kernel(x_ref, out_ref, got_c, part, got_r, send_r, recv_r, send_c, recv_c):
+    r, c, nr, nc = greet()
+    across, along = {}, []
+    for d in list(range(1, nr)) + [0]:
+        for e in range(1, nc):
+            slot = lax.rem(r + d, nr) * nc + lax.rem(c + e, nc)
+            copy = pltpu.make_async_remote_copy(
+                src_ref=x_ref.at[slot], dst_ref=got_c.at[d * nc + e],
+                send_sem=send_c.at[d * nc + e], recv_sem=recv_c.at[d * nc + e],
+                device_id={"col": lax.rem(c + e, nc)}, device_id_type=MESH)
+            copy.start()
+            across[d, e] = copy
+    for d in list(range(1, nr)) + [0]:
+        total = x_ref[lax.rem(r + d, nr) * nc + c]
+        for e in range(1, nc):
+            across[d, e].wait_recv()
+            total = total + got_c[d * nc + e]
+        part[d] = total
+        if d > 0:
+            copy = pltpu.make_async_remote_copy(
+                src_ref=part.at[d], dst_ref=got_r.at[d], send_sem=send_r.at[d], recv_sem=recv_r.at[d],
+                device_id={"row": lax.rem(r + d, nr)}, device_id_type=MESH)
+            copy.start()
+            along.append(copy)
+    total = part[0]
+    for d in range(1, nr):
+        along[d - 1].wait_recv()
+        total = total + got_r[d]
+    out_ref[...] = total
+    for copy in list(across.values()) + along:
+        copy.wait_send()
+
+
+def sems(nr, nc):
+    dma = pltpu.SemaphoreType.DMA
+    return [dma((nr,)), dma((nr,)), dma((nr * nc,)), dma((nr * nc,))]
+
+
 def gather(part):
-    return lax.all_gather(part, ("row", "col"), axis=0, tiled=True)
+    nr, nc = lax.axis_size("row"), lax.axis_size("col")
+    k, w, z = part.shape
+    out = pl.pallas_call(
+        gather_kernel,
+        in_specs=[pl.BlockSpec(memory_space=pltpu.VMEM)],
+        out_specs=pl.BlockSpec(memory_space=pltpu.VMEM),
+        out_shape=jax.ShapeDtypeStruct((nr * nc, k * w, z), jnp.float32),
+        scratch_shapes=sems(nr, nc),
+        compiler_params=pltpu.CompilerParams(collective_id=0, has_side_effects=True),
+    )(part.reshape(k * w, z))
+    return out.reshape(nr * nc * k, w, z)
 
 
 def scatter(part):
-    return lax.psum_scatter(part, ("row", "col"), scatter_dimension=0, tiled=True)
+    nr, nc = lax.axis_size("row"), lax.axis_size("col")
+    k, w, z = part.shape
+    size = (k // (nr * nc)) * w
+    block = lambda n: pltpu.VMEM((n, size, z), jnp.float32)
+    out = pl.pallas_call(
+        scatter_kernel,
+        in_specs=[pl.BlockSpec(memory_space=pltpu.VMEM)],
+        out_specs=pl.BlockSpec(memory_space=pltpu.VMEM),
+        out_shape=jax.ShapeDtypeStruct((size, z), jnp.float32),
+        scratch_shapes=[block(nr * nc), block(nr), block(nr)] + sems(nr, nc),
+        compiler_params=pltpu.CompilerParams(collective_id=1, has_side_effects=True),
+    )(part.reshape(nr * nc, size, z))
+    return out.reshape(k // (nr * nc), w, z)
 
 
 def other_waves(part):

time: 605 us -> 515 us (0.85)
  waiting for transfers between devices: 335 us -> 14.5 us
  Pallas kernels: 52.1 us -> 273 us
  local copies, waits for them, and re-layouts: 17.3 us -> 51.1 us
  starting transfers between devices: 64 us -> 49.2 us
  between operations: 14.6 us -> 1.33 us
  matrix products: 107 us -> 115 us
    pallas_call x0 -> x4, Pallas kernels: none -> 221 us  [the longest x2 116 us: gather(): pl.pallas_call(gather_kernel, in_specs=[pl.BlockSpec(memory_space=pltpu.V...]
    all_gather x2 -> x0, waiting for transfers between devices: 135 us -> none  [gather(): return lax.all_gather(part, ('row', 'col'), axis=0, tiled=True)]
    reduce_scatter x2 -> x0, waiting for transfers between devices: 99.7 us -> none  [scatter(): lax.psum_scatter(part, ('row', 'col'), scatter_dimension=0, tiled=True)]
    ppermute x8, waiting for transfers between devices: 78.4 us -> 0.02 us  [edges_of(): out.append(lax.ppermute(head, axis, [(i + 1, i) for i in range(count - 1)]))]
    reshape x0 -> x7, local copies, waits for them, and re-layouts: none -> 23.6 us  [the longest x2 10.6 us: scatter(): part.reshape(nr * nc, size, z)]
    ppermute x8, starting transfers between devices: 53.5 us -> 38.9 us  [edges_of(): out.append(lax.ppermute(tail, axis, [(i, i + 1) for i in range(count - 1)]))]
    transpose x0 -> x2, local copies, waits for them, and re-layouts: none -> 9.42 us  [per_device(): summed.append(scatter(jnp.einsum('kwc,wzc->kwz', left, c, precision=high)))]
    ppermute x8, waiting for transfers between devices: 7.86 us -> 0.02 us  [edges_of(): out.append(lax.ppermute(tail, axis, [(i, i + 1) for i in range(count - 1)]))]
  transfers between devices with their start and end apart: 22 -> 18, of which waited for: 12 -> 2; matrix products, arithmetic and copies ran while one was open for 1% -> 17% of each run, Pallas kernels for 3% -> 34%
where the time goes in v3:
time: 515 us; the launch traced here: 508 us
  Pallas kernels  273 us (53%)
  matrix products  115 us (22%)
  local copies, waits for them, and re-layouts  51.1 us (10%)
  starting transfers between devices  49.2 us (10%)
  waiting for transfers between devices  14.5 us (3%)
    pallas_call x2, Pallas kernels, gather(): pl.pallas_call(gather_kernel, in_specs=[pl.BlockSpec(memory_space=pltpu.V...  116 us
    pallas_call x2, Pallas kernels, scatter(): pl.pallas_call(scatter_kernel, in_specs=[pl.BlockSpec(memory_space=pltpu....  105 us
    ppermute x8, starting transfers between devices, edges_of(): out.append(lax.ppermute(tail, axis, [(i, i + 1) for i in range(count - 1)]))  38.9 us
    dot_general x2, matrix products, per_device(): left = jnp.einsum('wkr,rc->kwc', r, masked, precision=high)  35.3 us
    pallas_call x2, Pallas kernels, primal_step(): pl.pallas_call(primal_kernel, grid=(steps,), in_specs=[whole] * 6 + halo,...  33.4 us
    dot_general x2, matrix products, per_device(): jnp.einsum('wkr,kwc->rc', r, c, precision=high)  32.5 us
    dot_general x2, matrix products, per_device(): jnp.einsum('kwz,wzc->kwc', f, c, precision=high)  27.7 us
    dot_general x2, matrix products, per_device(): summed.append(scatter(jnp.einsum('kwc,wzc->kwz', left, c, precision=high)))  19.8 us
  transfers between devices with their start and end apart: 18, of which 2 were waited for; matrix products, arithmetic and copies ran while one was open for 17% of the time, Pallas kernels for 34%

profile of v3, /device:TPU:0, one launch (start us, length us, event | category | flops | bytes accessed | tf_op | source)
XLA Modules:
  0.0 508.0 jit_solution(1254611049385156811)
XLA Ops:
  2.7 5.6 %collective-permute-start = (f32[1,1024]{1,0:T(1,128)S(1)}, f32[1,1024]{1,0:T(1,128)S(1)}, u32[]{:S(2)}, u32[]{:S(2)}) collective-permute-start(f32[1,1024]{1,0:T(1,128)S(1)} %get-tuple-element.52), channel_id=1, source_target_pairs={{0,8},{8,16},{16,24},{1,9},{9,17},{17,25},{2,10},{10,18},{18,26},{... | collective-permute-start | bytes 12296 | tf_op jit(solution)/shard_map/ppermute | solution.py:99
  17.5 66.2 %shard_map.103 = f32[16,128,512]{2,1,0:T(8,128)} custom-call(f32[128,512]{1,0:T(8,128)} %reshape.30.x_ref), custom_call_target="tpu_custom_call" | custom-call | tf_op jit(solution)/shard_map/pallas_call | solution.py:186
  83.7 5.2 %reshape.31 = f32[512,4,512]{2,1,0:T(4,128)} reshape(f32[16,128,512]{2,1,0:T(8,128)} %shard_map.103) | data formatting | bytes 8388608 | tf_op jit(solution)/shard_map/reshape | solution.py:194
  88.9 13.9 %fusion.10 = f32[4,512,1024]{1,2,0:T(8,128)S(1)} fusion(f32[4,512,1024]{2,1,0:T(8,128)} %param.15, f32[512,4,512]{2,1,0:T(4,128)} %reshape.31), kind=kOutput, calls=%fused_computation.10 | convolution fusion | flops 6442450944 | bytes 20971520 | tf_op jit(solution)/shard_map/kwz,wzc->kwc/dot_general | solution.py:238
  102.9 16.3 %fusion.12.mine = f32[1024,1024]{1,0:T(8,128)S(1)} fusion(f32[4,512,1024]{2,1,0:T(8,128)} %param.14, f32[4,512,1024]{1,2,0:T(8,128)S(1)} %fusion.10), kind=kOutput, calls=%fused_computation.12 | convolution fusion | flops 12884901888 | bytes 20971520 | tf_op jit(solution)/shard_map/wkr,kwc->rc/dot_general | solution.py:240
  121.2 7.3 %collective-permute-done.4.other = f32[1024,1024]{1,0:T(8,128)} collective-permute-done((f32[1024,1024]{1,0:T(8,128)S(1)}, f32[1024,1024]{1,0:T(8,128)}, u32[]{:S(2)}, u32[]{:S(2)}) %collective-permute-start.4) | collective-permute-done | bytes 4194336 | tf_op jit(solution)/shard_map/ppermute | solution.py:218
  128.5 16.6 %shard_map.104 = (f32[1024,1024]{1,0:T(8,128)}, f32[1024,1024]{1,0:T(8,128)}, f32[1024,1024]{1,0:T(8,128)}) custom-call(f32[1024,1024]{1,0:T(8,128)} %copy-done.1, f32[1024,1024]{1,0:T(8,128)} %collective-permute-done.4.other, f32[1024,1024]{1,0:T(8,128)} %primal.1, s32[1024,1024]{1,0:T(8,128)} %pupil_m.3, s32[1024,1024]{1,0:T(8,128)} %lyot_m.3, ...), custom_call_target="tpu_custom_call" | custom-call | flops 31457280 | bytes 37748736 | tf_op jit(solution)/shard_map/pallas_call | solution.py:70
  159.5 18.3 %fusion.6 = f32[1024,4,512]{0,2,1:T(8,128)} fusion(f32[4,512,1024]{2,1,0:T(8,128)} %param.14, f32[1024,1024]{1,0:T(8,128)} %get-tuple-element.25), kind=kOutput, calls=%fused_computation.6 | convolution fusion | flops 12884901888 | bytes 20971520 | tf_op jit(solution)/shard_map/wkr,rc->kwc/dot_general | solution.py:248
  179.4 9.4 %shard_map.106.dual.above.below = f32[1024,1024]{1,0:T(8,128)} custom-call(f32[1024,1024]{1,0:T(8,128)} %dual.3, f32[1024,1024]{1,0:T(8,128)} %get-tuple-element.26.ext.above.below, f32[1024,1024]{1,0:T(8,128)} %get-tuple-element.26.ext.above.below, f32[1024,1024]{1,0:T(8,128)} %get-tuple-element.26.ext.above.below, f32[1,1024]{1,0:T(1,128)} %copy-done.20, ...), custom_call_target="tpu_custom_call" | custom-call | flops 20971520 | bytes 12582912 | tf_op jit(solution)/shard_map/pallas_call | solution.py:83
  198.1 5.4 %collective-permute-start.11 = (f32[1024,1]{1,0:T(8,128)S(1)}, f32[1024,1]{1,0:T(8,128)S(1)}, u32[]{:S(2)}, u32[]{:S(2)}) collective-permute-start(f32[1024,1]{1,0:T(8,128)S(1)} %get-tuple-element.42), channel_id=1, source_target_pairs={{0,2},{2,4},{4,6},{1,3},{3,5},{5,7},{8,10},{10,12},{12,14},{9,11},... | collective-permute-start | bytes 12296 | tf_op jit(solution)/shard_map/ppermute | solution.py:99
  203.6 10.5 %convolution_bitcast_fusion.1 = f32[512,4,512]{2,0,1:T(8,128)S(1)} fusion(f32[1024,4,512]{0,2,1:T(8,128)} %fusion.6, f32[4,512,1024]{2,1,0:T(8,128)} %param.15), kind=kOutput, calls=%fused_computation.15 | convolution fusion | flops 6442450944 | bytes 20971520 | tf_op jit(solution)/shard_map/kwc,wzc->kwz/dot_general | solution.py:249
  218.8 5.3 %reshape.32.x_ref = f32[16,128,512]{2,1,0:T(8,128)} reshape(f32[512,4,512]{2,1,0:T(4,128)} %copy.12) | data formatting | bytes 8388608 | tf_op jit(solution)/shard_map/reshape | solution.py:209
  224.1 52.3 %shard_map.105 = f32[128,512]{1,0:T(8,128)} custom-call(f32[16,128,512]{2,1,0:T(8,128)} %reshape.32.x_ref), custom_call_target="tpu_custom_call" | custom-call | tf_op jit(solution)/shard_map/pallas_call | solution.py:202
  278.6 50.1 %shard_map.107 = f32[16,128,512]{2,1,0:T(8,128)} custom-call(f32[128,512]{1,0:T(8,128)} %reshape.34.x_ref), custom_call_target="tpu_custom_call" | custom-call | tf_op jit(solution)/shard_map/pallas_call | solution.py:186
  328.7 5.2 %reshape.35 = f32[512,4,512]{2,1,0:T(4,128)} reshape(f32[16,128,512]{2,1,0:T(8,128)} %shard_map.107) | data formatting | bytes 8388608 | tf_op jit(solution)/shard_map/reshape | solution.py:194
  333.8 13.8 %fusion.8 = f32[4,512,1024]{1,2,0:T(8,128)S(1)} fusion(f32[4,512,1024]{2,1,0:T(8,128)} %param.15, f32[512,4,512]{2,1,0:T(4,128)} %reshape.35), kind=kOutput, calls=%fused_computation.8 | convolution fusion | flops 6442450944 | bytes 20971520 | tf_op jit(solution)/shard_map/kwz,wzc->kwc/dot_general | solution.py:238
  347.6 16.2 %fusion.15.mine = f32[1024,1024]{1,0:T(8,128)S(1)} fusion(f32[4,512,1024]{2,1,0:T(8,128)} %param.14, f32[4,512,1024]{1,2,0:T(8,128)S(1)} %fusion.8), kind=kOutput, calls=%fused_computation.13 | convolution fusion | flops 12884901888 | bytes 20971520 | tf_op jit(solution)/shard_map/wkr,kwc->rc/dot_general | solution.py:240
  365.9 7.2 %collective-permute-done.13.other = f32[1024,1024]{1,0:T(8,128)S(1)} collective-permute-done((f32[1024,1024]{1,0:T(8,128)S(1)}, f32[1024,1024]{1,0:T(8,128)S(1)}, u32[]{:S(2)}, u32[]{:S(2)}) %collective-permute-start.13) | collective-permute-done | bytes 4194336 | tf_op jit(solution)/shard_map/ppermute | solution.py:218
  375.1 16.8 %shard_map.108 = (f32[1024,1024]{1,0:T(8,128)}, f32[1024,1024]{1,0:T(8,128)}, f32[1024,1024]{1,0:T(8,128)}) custom-call(f32[1024,1024]{1,0:T(8,128)} %copy-done, f32[1024,1024]{1,0:T(8,128)} %copy-done.2, f32[1024,1024]{1,0:T(8,128)} %get-tuple-element.28.primal, s32[1024,1024]{1,0:T(8,128)} %pupil_m.3, s32[1024,1024]{1,0:T(8,128)} %lyot_m.3, ...), custom_call_target="tpu_custom_call" | custom-call | flops 31457280 | bytes 37748736 | tf_op jit(solution)/shard_map/pallas_call | solution.py:70
  405.8 17.0 %fusion.4 = f32[1024,4,512]{0,2,1:T(8,128)S(1)} fusion(f32[4,512,1024]{2,1,0:T(8,128)} %param.14, f32[1024,1024]{1,0:T(8,128)} %get-tuple-element.35), kind=kOutput, calls=%fused_computation.4 | convolution fusion | flops 12884901888 | bytes 20971520 | tf_op jit(solution)/shard_map/wkr,rc->kwc/dot_general | solution.py:248
  422.8 9.3 %convolution_bitcast_fusion = f32[512,4,512]{2,0,1:T(8,128)S(1)} fusion(f32[1024,4,512]{0,2,1:T(8,128)S(1)} %fusion.4, f32[4,512,1024]{2,1,0:T(8,128)} %param.15), kind=kOutput, calls=%fused_computation.14 | convolution fusion | flops 6442450944 | bytes 20971520 | tf_op jit(solution)/shard_map/kwc,wzc->kwz/dot_general | solution.py:249
  436.8 5.3 %reshape.36.x_ref = f32[16,128,512]{2,1,0:T(8,128)} reshape(f32[512,4,512]{2,1,0:T(4,128)} %copy.14) | data formatting | bytes 8388608 | tf_op jit(solution)/shard_map/reshape | solution.py:209
  442.1 52.6 %shard_map.109 = f32[128,512]{1,0:T(8,128)} custom-call(f32[16,128,512]{2,1,0:T(8,128)} %reshape.36.x_ref), custom_call_target="tpu_custom_call" | custom-call | tf_op jit(solution)/shard_map/pallas_call | solution.py:202
  498.4 9.4 %shard_map.110 = f32[1024,1024]{1,0:T(8,128)} custom-call(f32[1024,1024]{1,0:T(8,128)} %shard_map.106.dual.above.below, f32[1024,1024]{1,0:T(8,128)} %get-tuple-element.36.ext.above.below, f32[1024,1024]{1,0:T(8,128)} %get-tuple-element.36.ext.above.below, f32[1024,1024]{1,0:T(8,128)} %get-tuple-element.36.ext.above.below, f32[1,1024]{1,0:T(1,128)} %copy-done.18, ...), custom_call_target="tpu_custom_call" | custom-call | flops 20971520 | bytes 12582912 | tf_op jit(solution)/shard_map/pallas_call | solution.py:83
  (92 shorter events, 71.5 us)
Async XLA Ops:
  1.4 87.4 %collective-permute-start.1 = (f32[1,1024]{1,0:T(1,128)S(1)}, f32[1,1024]{1,0:T(1,128)S(1)}, u32[]{:S(2)}, u32[]{:S(2)}) collective-permute-start(f32[1,1024]{1,0:T(1,128)S(1)} %get-tuple-element.51), channel_id=1, source_target_pairs={{8,0},{16,8},{24,16},{9,1},{17,9},{25,17},{10,2},{18,10},{26,18},{... | collective-permute-start | bytes 12296 | tf_op jit(solution)/shard_map/ppermute | solution.py:100
  2.7 86.2 %collective-permute-start = (f32[1,1024]{1,0:T(1,128)S(1)}, f32[1,1024]{1,0:T(1,128)S(1)}, u32[]{:S(2)}, u32[]{:S(2)}) collective-permute-start(f32[1,1024]{1,0:T(1,128)S(1)} %get-tuple-element.52), channel_id=1, source_target_pairs={{0,8},{8,16},{16,24},{1,9},{9,17},{17,25},{2,10},{10,18},{18,26},{... | collective-permute-start | bytes 12296 | tf_op jit(solution)/shard_map/ppermute | solution.py:99
  9.7 79.2 %collective-permute-start.3 = (f32[1024,1]{1,0:T(8,128)S(1)}, f32[1024,1]{1,0:T(8,128)S(1)}, u32[]{:S(2)}, u32[]{:S(2)}) collective-permute-start(f32[1024,1]{1,0:T(8,128)S(1)} %get-tuple-element.49), channel_id=1, source_target_pairs={{2,0},{4,2},{6,4},{3,1},{5,3},{7,5},{10,8},{12,10},{14,12},{11,9},... | collective-permute-start | bytes 12296 | tf_op jit(solution)/shard_map/ppermute | solution.py:100
  11.0 77.9 %collective-permute-start.2 = (f32[1024,1]{1,0:T(8,128)S(1)}, f32[1024,1]{1,0:T(8,128)S(1)}, u32[]{:S(2)}, u32[]{:S(2)}) collective-permute-start(f32[1024,1]{1,0:T(8,128)S(1)} %get-tuple-element.50), channel_id=1, source_target_pairs={{0,2},{2,4},{4,6},{1,3},{3,5},{5,7},{8,10},{10,12},{12,14},{9,11},... | collective-permute-start | bytes 12296 | tf_op jit(solution)/shard_map/ppermute | solution.py:99
  121.2 7.3 %collective-permute-start.4 = (f32[1024,1024]{1,0:T(8,128)S(1)}, f32[1024,1024]{1,0:T(8,128)}, u32[]{:S(2)}, u32[]{:S(2)}) collective-permute-start(f32[1024,1024]{1,0:T(8,128)S(1)} %fusion.12.mine), channel_id=1, source_target_pairs={{0,1},{1,0},{2,3},{3,2},{4,5},{5,4},{6,7},{7,6},{8,9},{9,8},{10,11... | collective-permute-start | bytes 12582920 | tf_op jit(solution)/shard_map/ppermute | solution.py:218
  147.3 30.5 %collective-permute-start.6 = (f32[1,1024]{1,0:T(1,128)S(1)}, f32[1,1024]{1,0:T(1,128)S(1)}, u32[]{:S(2)}, u32[]{:S(2)}) collective-permute-start(f32[1,1024]{1,0:T(1,128)S(1)} %get-tuple-element.47), channel_id=1, source_target_pairs={{8,0},{16,8},{24,16},{9,1},{17,9},{25,17},{10,2},{18,10},{26,18},{... | collective-permute-start | bytes 12296 | tf_op jit(solution)/shard_map/ppermute | solution.py:100
  148.6 29.2 %collective-permute-start.5 = (f32[1,1024]{1,0:T(1,128)S(1)}, f32[1,1024]{1,0:T(1,128)S(1)}, u32[]{:S(2)}, u32[]{:S(2)}) collective-permute-start(f32[1,1024]{1,0:T(1,128)S(1)} %get-tuple-element.48), channel_id=1, source_target_pairs={{0,8},{8,16},{16,24},{1,9},{9,17},{17,25},{2,10},{10,18},{18,26},{... | collective-permute-start | bytes 12296 | tf_op jit(solution)/shard_map/ppermute | solution.py:99
  153.1 24.7 %collective-permute-start.8 = (f32[1024,1]{1,0:T(8,128)S(1)}, f32[1024,1]{1,0:T(8,128)S(1)}, u32[]{:S(2)}, u32[]{:S(2)}) collective-permute-start(f32[1024,1]{1,0:T(8,128)S(1)} %get-tuple-element.45), channel_id=1, source_target_pairs={{2,0},{4,2},{6,4},{3,1},{5,3},{7,5},{10,8},{12,10},{14,12},{11,9},... | collective-permute-start | bytes 12296 | tf_op jit(solution)/shard_map/ppermute | solution.py:100
  154.4 23.4 %collective-permute-start.7 = (f32[1024,1]{1,0:T(8,128)S(1)}, f32[1024,1]{1,0:T(8,128)S(1)}, u32[]{:S(2)}, u32[]{:S(2)}) collective-permute-start(f32[1024,1]{1,0:T(8,128)S(1)} %get-tuple-element.46), channel_id=1, source_target_pairs={{0,2},{2,4},{4,6},{1,3},{3,5},{5,7},{8,10},{10,12},{12,14},{9,11},... | collective-permute-start | bytes 12296 | tf_op jit(solution)/shard_map/ppermute | solution.py:99
  191.0 86.5 %collective-permute-start.10 = (f32[1,1024]{1,0:T(1,128)S(1)}, f32[1,1024]{1,0:T(1,128)S(1)}, u32[]{:S(2)}, u32[]{:S(2)}) collective-permute-start(f32[1,1024]{1,0:T(1,128)S(1)} %get-tuple-element.43), channel_id=1, source_target_pairs={{8,0},{16,8},{24,16},{9,1},{17,9},{25,17},{10,2},{18,10},{26,18},{... | collective-permute-start | bytes 12296 | tf_op jit(solution)/shard_map/ppermute | solution.py:100
  192.3 85.2 %collective-permute-start.9 = (f32[1,1024]{1,0:T(1,128)S(1)}, f32[1,1024]{1,0:T(1,128)S(1)}, u32[]{:S(2)}, u32[]{:S(2)}) collective-permute-start(f32[1,1024]{1,0:T(1,128)S(1)} %get-tuple-element.44), channel_id=1, source_target_pairs={{0,8},{8,16},{16,24},{1,9},{9,17},{17,25},{2,10},{10,18},{18,26},{... | collective-permute-start | bytes 12296 | tf_op jit(solution)/shard_map/ppermute | solution.py:99
  196.8 80.7 %collective-permute-start.12 = (f32[1024,1]{1,0:T(8,128)S(1)}, f32[1024,1]{1,0:T(8,128)S(1)}, u32[]{:S(2)}, u32[]{:S(2)}) collective-permute-start(f32[1024,1]{1,0:T(8,128)S(1)} %get-tuple-element.41), channel_id=1, source_target_pairs={{2,0},{4,2},{6,4},{3,1},{5,3},{7,5},{10,8},{12,10},{14,12},{11,9},... | collective-permute-start | bytes 12296 | tf_op jit(solution)/shard_map/ppermute | solution.py:100
  198.1 79.4 %collective-permute-start.11 = (f32[1024,1]{1,0:T(8,128)S(1)}, f32[1024,1]{1,0:T(8,128)S(1)}, u32[]{:S(2)}, u32[]{:S(2)}) collective-permute-start(f32[1024,1]{1,0:T(8,128)S(1)} %get-tuple-element.42), channel_id=1, source_target_pairs={{0,2},{2,4},{4,6},{1,3},{3,5},{5,7},{8,10},{10,12},{12,14},{9,11},... | collective-permute-start | bytes 12296 | tf_op jit(solution)/shard_map/ppermute | solution.py:99
  224.1 53.5 %copy-start.3 = (s32[32,4,512]{2,1,0:T(4,128)S(1)}, s32[32,4,512]{2,1,0:T(4,128)}, u32[]{:S(2)}) copy-start(s32[32,4,512]{2,1,0:T(4,128)} %param.13) | copy-start | bytes 786436
  224.1 53.5 %copy-start.4 = (f32[32,4,512]{2,1,0:T(4,128)S(1)}, f32[32,4,512]{2,1,0:T(4,128)}, u32[]{:S(2)}) copy-start(f32[32,4,512]{2,1,0:T(4,128)} %param.9) | copy-start | bytes 786436
  277.5 56.4 %copy-start.13 = (f32[1,1024]{1,0:T(1,128)}, f32[1,1024]{1,0:T(1,128)S(1)}, u32[]{:S(2)}) copy-start(f32[1,1024]{1,0:T(1,128)S(1)} %collective-permute-done.10.bottom) | copy-start | bytes 12292
  277.5 56.3 %copy-start.14 = (f32[1,1024]{1,0:T(1,128)}, f32[1,1024]{1,0:T(1,128)S(1)}, u32[]{:S(2)}) copy-start(f32[1,1024]{1,0:T(1,128)S(1)} %collective-permute-done.9.top) | copy-start | bytes 12292
  277.5 56.3 %copy-start.5 = (f32[1024,1]{1,0:T(8,128)}, f32[1024,1]{1,0:T(8,128)S(1)}, u32[]{:S(2)}) copy-start(f32[1024,1]{1,0:T(8,128)S(1)} %collective-permute-done.12.right) | copy-start | bytes 12292
  277.5 56.3 %copy-start.6 = (f32[1024,1]{1,0:T(8,128)}, f32[1024,1]{1,0:T(8,128)S(1)}, u32[]{:S(2)}) copy-start(f32[1024,1]{1,0:T(8,128)S(1)} %collective-permute-done.11.left) | copy-start | bytes 12292
  365.9 7.2 %collective-permute-start.13 = (f32[1024,1024]{1,0:T(8,128)S(1)}, f32[1024,1024]{1,0:T(8,128)S(1)}, u32[]{:S(2)}, u32[]{:S(2)}) collective-permute-start(f32[1024,1024]{1,0:T(8,128)S(1)} %fusion.15.mine), channel_id=1, source_target_pairs={{0,1},{1,0},{2,3},{3,2},{4,5},{5,4},{6,7},{7,6},{8,9},{9,8},{10,11... | collective-permute-start | bytes 12582920 | tf_op jit(solution)/shard_map/ppermute | solution.py:218
  394.0 102.7 %collective-permute-start.15 = (f32[1,1024]{1,0:T(1,128)S(1)}, f32[1,1024]{1,0:T(1,128)S(1)}, u32[]{:S(2)}, u32[]{:S(2)}) collective-permute-start(f32[1,1024]{1,0:T(1,128)S(1)} %get-tuple-element.39), channel_id=1, source_target_pairs={{8,0},{16,8},{24,16},{9,1},{17,9},{25,17},{10,2},{18,10},{26,18},{... | collective-permute-start | bytes 12296 | tf_op jit(solution)/shard_map/ppermute | solution.py:100
  395.3 101.4 %collective-permute-start.14 = (f32[1,1024]{1,0:T(1,128)S(1)}, f32[1,1024]{1,0:T(1,128)S(1)}, u32[]{:S(2)}, u32[]{:S(2)}) collective-permute-start(f32[1,1024]{1,0:T(1,128)S(1)} %get-tuple-element.40), channel_id=1, source_target_pairs={{0,8},{8,16},{16,24},{1,9},{9,17},{17,25},{2,10},{10,18},{18,26},{... | collective-permute-start | bytes 12296 | tf_op jit(solution)/shard_map/ppermute | solution.py:99
  399.9 96.8 %collective-permute-start.17 = (f32[1024,1]{1,0:T(8,128)S(1)}, f32[1024,1]{1,0:T(8,128)S(1)}, u32[]{:S(2)}, u32[]{:S(2)}) collective-permute-start(f32[1024,1]{1,0:T(8,128)S(1)} %get-tuple-element.37), channel_id=1, source_target_pairs={{2,0},{4,2},{6,4},{3,1},{5,3},{7,5},{10,8},{12,10},{14,12},{11,9},... | collective-permute-start | bytes 12296 | tf_op jit(solution)/shard_map/ppermute | solution.py:100
  401.2 95.5 %collective-permute-start.16 = (f32[1024,1]{1,0:T(8,128)S(1)}, f32[1024,1]{1,0:T(8,128)S(1)}, u32[]{:S(2)}, u32[]{:S(2)}) collective-permute-start(f32[1024,1]{1,0:T(8,128)S(1)} %get-tuple-element.38), channel_id=1, source_target_pairs={{0,2},{2,4},{4,6},{1,3},{3,5},{5,7},{8,10},{10,12},{12,14},{9,11},... | collective-permute-start | bytes 12296 | tf_op jit(solution)/shard_map/ppermute | solution.py:99
  (15 other events, 67.6 us)
